TPU v7x, 32 devices: a whole 2x2x4 slice. The times are simulated.
32 devices in a mesh: clips: 2 (over y), tiles: 4 (over z), frames: 2 (over x), chan: 2 (over core).
Axes of the slice: x: 2, y: 2, z: 4, core: 2. Of those that a mesh axis runs over, the one named last changes fastest.
Arguments:
- lr_feats: bfloat16 [8, 2, 64, 32, 128], P('clips', 'frames', 'chan', 'tiles'), parts along dimension 0, may hold values from -6 to 6
- flow_prev: int32 [8, 2, 4, 2], P('clips', None, 'tiles'), parts along dimension 0, may hold values from -8 to 8, as said below
- flow_second: int32 [8, 2, 4, 2], P('clips', None, 'tiles'), parts along dimension 0, may hold values from -8 to 8, as said below
- w_join: bfloat16 [9, 64, 192], P(None, 'chan'), may hold values from -0.15625 to 0.15625
- b_join: float32 [64], P('chan'), may hold values from -3 to 3
- w_first: bfloat16 [1, 9, 64, 64], P(None, None, 'chan'), may hold values from -0.25 to 0.25
- b_first: float32 [1, 64], P(None, 'chan'), may hold values from -3 to 3
- w_second: bfloat16 [1, 9, 64, 64], P(None, None, 'chan'), may hold values from -0.25 to 0.25
- b_second: float32 [1, 64], P(None, 'chan'), may hold values from -3 to 3
Outputs:
- hidden: bfloat16 [8, 2, 64, 32, 128], P('clips', 'frames', 'chan', 'tiles'), parts along dimension 0
There are 2 independent parts, one for each index of `clips`. A program takes and returns all parts, laid end to end along the dimension named above; an argument that names none is the same for every part. Nothing has to cross between parts.
Inputs may be any that keep to these rules, and one draw needn't show every extreme that they name: `flow_prev`: both entries (dy, dx) of every block lie in the range; +8 and -8 each occur in every draw. `flow_second`: both entries (dy, dx) of every block lie in the range; +8 and -8 each occur in every draw.
All inputs are finite; a program needn't handle non-finite values.
Results may differ from a plain program's by a relative error of at most 0.012.
Values may be sent and summed in bfloat16 or wider, within the bound.
No kernel may reach another device: no remote copies, remote signals or barrier semaphores. Data moves between devices by JAX's collectives and lax.ppermute only.
A program may use at most 64 MiB of HBM per device.

v0:
```python
import jax
import jax.numpy as jnp
from jax import lax
from jax.sharding import PartitionSpec as P

BH = 8


def padded_2(array, sides, width):
    for axis, dim in sides:
        devices, length = (lax.axis_size(axis), array.shape[dim])
        up = [(i, (i + 1) % devices) for i in range(devices - 1)]
        down = [(j, i) for i, j in up]
        last = lax.slice_in_dim(array, length - width, length, axis=dim)
        first = lax.slice_in_dim(array, 0, width, axis=dim)
        before = lax.ppermute(last, axis, up)
        after = lax.ppermute(first, axis, down)
        array = jnp.concatenate([before, array, after], axis=dim)
    return array


def for_sending(array):
    return jax.tree.map(lambda a: a.astype(jnp.bfloat16) if a.dtype == jnp.float32 else a, array)


def shifted(block, axis, distance):
    devices = range(lax.axis_size(axis))
    route = [(i - distance, i) for i in devices if i - distance in devices]
    return lax.ppermute(block, axis, route)


def displace(rimmed, offsets, tile_rows):
    channels = rimmed.shape[0]
    col_count = rimmed.shape[2]
    padded = jnp.pad(rimmed, ((0, 0), (0, 0), (tile_rows, tile_rows)))
    start_row = tile_rows + offsets[0, 0]
    start_col = tile_rows + offsets[0, 1]
    pieces = [lax.dynamic_slice(padded, (0, start_row, start_col), (channels, BH, col_count))]
    return jnp.concatenate(pieces, axis=1)


def convolve_rows(inputs, weights, bias_vec):
    in_count, row_count, col_count = inputs.shape
    rimmed = padded_2(inputs, (("tiles", 1),), 1)
    padded = jnp.pad(rimmed, ((0, 0), (0, 0), (1, 1)))
    total_sum = jnp.zeros((weights.shape[1], row_count * col_count), jnp.float32)
    for tap_index in range(9):
        tap_row = tap_index // 3
        tap_col = tap_index % 3
        window = padded[:, tap_row : tap_row + row_count, tap_col : tap_col + col_count].reshape(
            in_count, row_count * col_count
        )
        total_sum = total_sum + jnp.dot(
            weights[tap_index], window, preferred_element_type=jnp.float32
        )
    return total_sum.reshape(-1, row_count, col_count) + bias_vec[:, None, None]


def block_conv(own_part, weights, bias_vec):
    whole_input = lax.all_gather(own_part, "chan", axis=0, tiled=True)
    return convolve_rows(whole_input, weights, bias_vec)


def refine(current, warped_one, warped_two, w_join, b_join, w_first, b_first, w_second, b_second):
    full_current, full_one, full_two = (
        lax.all_gather(current, "chan", axis=0, tiled=True),
        lax.all_gather(warped_one, "chan", axis=0, tiled=True),
        lax.all_gather(warped_two, "chan", axis=0, tiled=True),
    )
    stacked = jnp.concatenate([full_current, full_one, full_two], axis=0)
    joined_sum = convolve_rows(stacked, w_join, b_join)
    joined_state = jnp.where(joined_sum > 0, joined_sum, 0.1 * joined_sum).astype(jnp.bfloat16)
    inner_act = jnp.maximum(block_conv(joined_state, w_first[0], b_first[0]), 0.0).astype(
        jnp.bfloat16
    )
    joined_state = (
        joined_state.astype(jnp.float32) + block_conv(inner_act, w_second[0], b_second[0])
    ).astype(jnp.bfloat16)
    return joined_state


def shards(lr_feats, flow_prev, flow_second, w_join, b_join, w_first, b_first, w_second, b_second):
    segments = lr_feats.shape[0]
    tile_rows = lr_feats.shape[3]
    frames_all = flow_prev.shape[1]
    owners = lax.axis_size("frames")
    position = lax.axis_index("frames")
    blank_feat = jnp.zeros(lr_feats.shape[2:], lr_feats.dtype)

    def advance(turn_index, carried):
        results, first_in, second_in, second_wait = carried
        segment = turn_index - position
        is_valid = (segment >= 0) & (segment < segments)
        seg_clip = jnp.clip(segment, 0, segments - 1)
        current = lax.dynamic_index_in_dim(lr_feats, seg_clip, 0, keepdims=False)[0]
        fresh_state = refine(
            current, first_in, second_in, w_join, b_join, w_first, b_first, w_second, b_second
        )
        kept_slice = lax.dynamic_index_in_dim(results, seg_clip, 0, keepdims=True)
        chosen = jnp.where(is_valid, fresh_state[None, None], kept_slice)
        results = lax.dynamic_update_index_in_dim(results, chosen[0], seg_clip, 0)
        rimmed_own = padded_2(fresh_state, (("tiles", 1),), tile_rows)
        frame_next = jnp.minimum(position + 1, frames_all - 1)
        frame_after = jnp.minimum(position + 2, frames_all - 1)
        ahead_one = displace(rimmed_own, flow_prev[seg_clip, frame_next], tile_rows)
        ahead_two = displace(rimmed_own, flow_second[seg_clip, frame_after], tile_rows)
        first_next = shifted(for_sending(ahead_one), "frames", 1).astype(ahead_one.dtype)
        wait_next = shifted(for_sending(ahead_two), "frames", 2).astype(ahead_two.dtype)
        return (results, first_next, second_wait, wait_next)

    initial = (jnp.zeros_like(lr_feats), blank_feat, blank_feat, blank_feat)
    results, first_in, second_in, second_wait = lax.fori_loop(
        0, segments + owners - 1, advance, initial
    )
    return results


def solution(mesh):
    in_specs = (
        P("clips", "frames", "chan", "tiles", None),
        P("clips", None, "tiles", None),
        P("clips", None, "tiles", None),
        P(None, "chan", None),
        P("chan"),
        P(None, None, "chan", None),
        P(None, "chan"),
        P(None, None, "chan", None),
        P(None, "chan"),
    )
    out_specs = P("clips", "frames", "chan", "tiles", None)
    return jax.shard_map(shards, mesh=mesh, in_specs=in_specs, out_specs=out_specs, check_vma=False)
```

profile of v0, /device:TPU:0, one launch (start us, length us, event | category | flops | bytes accessed | tf_op | source)
XLA Modules:
  0.0 324.6 jit_solution(14142174977703277329)
XLA Ops:
  1.6 322.3 %while.22 = (s32[]{:T(128)}, bf16[4,1,32,8,128]{4,3,2,1,0:T(8,128)(2,1)S(1)}, bf16[32,8,128]{2,1,0:T(8,128)(2,1)S(1)}, bf16[32,8,128]{2,1,0:T(8,128)(2,1)S(1)}, ...) while((s32[]{:T(128)}, ...), condition=%wide.region_1.2_spmd, body=%wide.region_0.1_spmd.sunk | while | flops 202819072 | bytes 31908440 | solution.py:112
  2.5 2.0 all-gather.2
  4.5 1.9 all_gather.59
  6.4 1.9 all_gather.60
  9.8 5.5 %collective-permute-start.1 = (bf16[192,1,128]{2,1,0:T(2,128)(2,1)S(1)}, bf16[192,1,128]{2,1,0:T(2,128)(2,1)S(1)}, u32[]{:S(2)}, u32[]{:S(2)}) collective-permute-start(bf16[192,1,128]{2,1,0:T(2,128)(2,1)S(1)} %get-tuple-element.690), channel_id=1, source_target_pairs={{0,4},{4,8},{8,12},{1,5},{5,9},{9,13},{2,6},{6,10},{10,14},{3,7},{... | collective-permute-start | bytes 147464 | tf_op jit(solution)/shard_map/while/body/eval_jaxpr/ppermute | solution.py:16
  17.6 4.1 %select_maximum_fusion.6 = bf16[192,10,130]{2,1,0:T(8,128)(2,1)S(1)} fusion(bf16[192,1,128]{2,1,0:T(2,128)(2,1)S(1)} %collective-permute-done, bf16[192,1,128]{2,1,0:T(2,128)(2,1)S(1)} %collective-permute-done.1, bf16[64,8,128]{2,1,0:T(8,128)(2,1)S(1)} %all_gather.59, bf16[64,8,128]{2,1,0:T(8,128)(2,1)S(1)} %all_gather.60, ...), kind=kLoop, calls=%fused_computation.5.clone.1 | loop fusion | flops 4492800 | bytes 990720 | tf_op jit(solution)/shard_map/while/body/eval_jaxpr/concatenate | solution.py:18
  24.9 1.9 all_gather.61
  28.1 5.0 %collective-permute-start.3 = (bf16[64,1,128]{2,1,0:T(2,128)(2,1)S(1)}, bf16[64,1,128]{2,1,0:T(2,128)(2,1)S(1)}, u32[]{:S(2)}, u32[]{:S(2)}) collective-permute-start(bf16[64,1,128]{2,1,0:T(2,128)(2,1)S(1)} %get-tuple-element.700), channel_id=1, source_target_pairs={{0,4},{4,8},{8,12},{1,5},{5,9},{9,13},{2,6},{6,10},{10,14},{3,7},{... | collective-permute-start | bytes 49160 | tf_op jit(solution)/shard_map/while/body/eval_jaxpr/ppermute | solution.py:16
  37.2 1.9 all_gather.62
  40.4 4.9 %collective-permute-start.5 = (bf16[64,1,128]{2,1,0:T(2,128)(2,1)S(1)}, bf16[64,1,128]{2,1,0:T(2,128)(2,1)S(1)}, u32[]{:S(2)}, u32[]{:S(2)}) collective-permute-start(bf16[64,1,128]{2,1,0:T(2,128)(2,1)S(1)} %get-tuple-element.710), channel_id=1, source_target_pairs={{0,4},{4,8},{8,12},{1,5},{5,9},{9,13},{2,6},{6,10},{10,14},{3,7},{... | collective-permute-start | bytes 49160 | tf_op jit(solution)/shard_map/while/body/eval_jaxpr/ppermute | solution.py:16
  50.8 4.6 %collective-permute-start.7 = (bf16[32,8,128]{2,1,0:T(8,128)(2,1)S(1)}, bf16[32,8,128]{2,1,0:T(8,128)(2,1)S(1)}, u32[]{:S(2)}, u32[]{:S(2)}) collective-permute-start(bf16[32,8,128]{2,1,0:T(8,128)(2,1)S(1)} %fusion.295), channel_id=1, source_target_pairs={{0,4},{4,8},{8,12},{1,5},{5,9},{9,13},{2,6},{6,10},{10,14},{3,7},{... | collective-permute-start | bytes 196616 | tf_op jit(solution)/shard_map/while/body/eval_jaxpr/ppermute | solution.py:16
  60.9 3.6 %collective-permute-start.8 = (bf16[32,8,128]{2,1,0:T(8,128)(2,1)S(1)}, bf16[32,8,128]{2,1,0:T(8,128)(2,1)S(1)}, u32[]{:S(2)}, u32[]{:S(2)}) collective-permute-start(bf16[32,8,128]{2,1,0:T(8,128)(2,1)S(1)} %get-tuple-element.725), channel_id=1, source_target_pairs={{0,2},{1,3},{4,6},{5,7},{8,10},{9,11},{12,14},{13,15},{16,18},{17,... | collective-permute-start | bytes 196616 | tf_op jit(solution)/shard_map/while/body/eval_jaxpr/ppermute | solution.py:29
  74.4 4.6 %collective-permute-start.1 = (bf16[192,1,128]{2,1,0:T(2,128)(2,1)S(1)}, bf16[192,1,128]{2,1,0:T(2,128)(2,1)S(1)}, u32[]{:S(2)}, u32[]{:S(2)}) collective-permute-start(bf16[192,1,128]{2,1,0:T(2,128)(2,1)S(1)} %get-tuple-element.690), channel_id=1, source_target_pairs={{0,4},{4,8},{8,12},{1,5},{5,9},{9,13},{2,6},{6,10},{10,14},{3,7},{... | collective-permute-start | bytes 147464 | tf_op jit(solution)/shard_map/while/body/eval_jaxpr/ppermute | solution.py:16
  81.3 4.1 %select_maximum_fusion.6 = bf16[192,10,130]{2,1,0:T(8,128)(2,1)S(1)} fusion(bf16[192,1,128]{2,1,0:T(2,128)(2,1)S(1)} %collective-permute-done, bf16[192,1,128]{2,1,0:T(2,128)(2,1)S(1)} %collective-permute-done.1, bf16[64,8,128]{2,1,0:T(8,128)(2,1)S(1)} %all_gather.59, bf16[64,8,128]{2,1,0:T(8,128)(2,1)S(1)} %all_gather.60, ...), kind=kLoop, calls=%fused_computation.5.clone.1 | loop fusion | flops 4492800 | bytes 990720 | tf_op jit(solution)/shard_map/while/body/eval_jaxpr/concatenate | solution.py:18
  88.6 1.9 all_gather.61
  91.8 5.0 %collective-permute-start.3 = (bf16[64,1,128]{2,1,0:T(2,128)(2,1)S(1)}, bf16[64,1,128]{2,1,0:T(2,128)(2,1)S(1)}, u32[]{:S(2)}, u32[]{:S(2)}) collective-permute-start(bf16[64,1,128]{2,1,0:T(2,128)(2,1)S(1)} %get-tuple-element.700), channel_id=1, source_target_pairs={{0,4},{4,8},{8,12},{1,5},{5,9},{9,13},{2,6},{6,10},{10,14},{3,7},{... | collective-permute-start | bytes 49160 | tf_op jit(solution)/shard_map/while/body/eval_jaxpr/ppermute | solution.py:16
  100.9 1.9 all_gather.62
  104.1 4.9 %collective-permute-start.5 = (bf16[64,1,128]{2,1,0:T(2,128)(2,1)S(1)}, bf16[64,1,128]{2,1,0:T(2,128)(2,1)S(1)}, u32[]{:S(2)}, u32[]{:S(2)}) collective-permute-start(bf16[64,1,128]{2,1,0:T(2,128)(2,1)S(1)} %get-tuple-element.710), channel_id=1, source_target_pairs={{0,4},{4,8},{8,12},{1,5},{5,9},{9,13},{2,6},{6,10},{10,14},{3,7},{... | collective-permute-start | bytes 49160 | tf_op jit(solution)/shard_map/while/body/eval_jaxpr/ppermute | solution.py:16
  114.5 4.6 %collective-permute-start.7 = (bf16[32,8,128]{2,1,0:T(8,128)(2,1)S(1)}, bf16[32,8,128]{2,1,0:T(8,128)(2,1)S(1)}, u32[]{:S(2)}, u32[]{:S(2)}) collective-permute-start(bf16[32,8,128]{2,1,0:T(8,128)(2,1)S(1)} %fusion.295), channel_id=1, source_target_pairs={{0,4},{4,8},{8,12},{1,5},{5,9},{9,13},{2,6},{6,10},{10,14},{3,7},{... | collective-permute-start | bytes 196616 | tf_op jit(solution)/shard_map/while/body/eval_jaxpr/ppermute | solution.py:16
  124.6 4.3 %collective-permute-start.8 = (bf16[32,8,128]{2,1,0:T(8,128)(2,1)S(1)}, bf16[32,8,128]{2,1,0:T(8,128)(2,1)S(1)}, u32[]{:S(2)}, u32[]{:S(2)}) collective-permute-start(bf16[32,8,128]{2,1,0:T(8,128)(2,1)S(1)} %get-tuple-element.725), channel_id=1, source_target_pairs={{0,2},{1,3},{4,6},{5,7},{8,10},{9,11},{12,14},{13,15},{16,18},{17,... | collective-permute-start | bytes 196616 | tf_op jit(solution)/shard_map/while/body/eval_jaxpr/ppermute | solution.py:29
  133.5 1.9 all_gather.59
  135.4 1.9 all_gather.60
  138.8 4.6 %collective-permute-start.1 = (bf16[192,1,128]{2,1,0:T(2,128)(2,1)S(1)}, bf16[192,1,128]{2,1,0:T(2,128)(2,1)S(1)}, u32[]{:S(2)}, u32[]{:S(2)}) collective-permute-start(bf16[192,1,128]{2,1,0:T(2,128)(2,1)S(1)} %get-tuple-element.690), channel_id=1, source_target_pairs={{0,4},{4,8},{8,12},{1,5},{5,9},{9,13},{2,6},{6,10},{10,14},{3,7},{... | collective-permute-start | bytes 147464 | tf_op jit(solution)/shard_map/while/body/eval_jaxpr/ppermute | solution.py:16
  145.7 4.1 %select_maximum_fusion.6 = bf16[192,10,130]{2,1,0:T(8,128)(2,1)S(1)} fusion(bf16[192,1,128]{2,1,0:T(2,128)(2,1)S(1)} %collective-permute-done, bf16[192,1,128]{2,1,0:T(2,128)(2,1)S(1)} %collective-permute-done.1, bf16[64,8,128]{2,1,0:T(8,128)(2,1)S(1)} %all_gather.59, bf16[64,8,128]{2,1,0:T(8,128)(2,1)S(1)} %all_gather.60, ...), kind=kLoop, calls=%fused_computation.5.clone.1 | loop fusion | flops 4492800 | bytes 990720 | tf_op jit(solution)/shard_map/while/body/eval_jaxpr/concatenate | solution.py:18
  153.0 1.9 all_gather.61
  156.2 5.0 %collective-permute-start.3 = (bf16[64,1,128]{2,1,0:T(2,128)(2,1)S(1)}, bf16[64,1,128]{2,1,0:T(2,128)(2,1)S(1)}, u32[]{:S(2)}, u32[]{:S(2)}) collective-permute-start(bf16[64,1,128]{2,1,0:T(2,128)(2,1)S(1)} %get-tuple-element.700), channel_id=1, source_target_pairs={{0,4},{4,8},{8,12},{1,5},{5,9},{9,13},{2,6},{6,10},{10,14},{3,7},{... | collective-permute-start | bytes 49160 | tf_op jit(solution)/shard_map/while/body/eval_jaxpr/ppermute | solution.py:16
  165.3 1.9 all_gather.62
  168.5 4.9 %collective-permute-start.5 = (bf16[64,1,128]{2,1,0:T(2,128)(2,1)S(1)}, bf16[64,1,128]{2,1,0:T(2,128)(2,1)S(1)}, u32[]{:S(2)}, u32[]{:S(2)}) collective-permute-start(bf16[64,1,128]{2,1,0:T(2,128)(2,1)S(1)} %get-tuple-element.710), channel_id=1, source_target_pairs={{0,4},{4,8},{8,12},{1,5},{5,9},{9,13},{2,6},{6,10},{10,14},{3,7},{... | collective-permute-start | bytes 49160 | tf_op jit(solution)/shard_map/while/body/eval_jaxpr/ppermute | solution.py:16
  178.9 4.6 %collective-permute-start.7 = (bf16[32,8,128]{2,1,0:T(8,128)(2,1)S(1)}, bf16[32,8,128]{2,1,0:T(8,128)(2,1)S(1)}, u32[]{:S(2)}, u32[]{:S(2)}) collective-permute-start(bf16[32,8,128]{2,1,0:T(8,128)(2,1)S(1)} %fusion.295), channel_id=1, source_target_pairs={{0,4},{4,8},{8,12},{1,5},{5,9},{9,13},{2,6},{6,10},{10,14},{3,7},{... | collective-permute-start | bytes 196616 | tf_op jit(solution)/shard_map/while/body/eval_jaxpr/ppermute | solution.py:16
  189.0 4.3 %collective-permute-start.8 = (bf16[32,8,128]{2,1,0:T(8,128)(2,1)S(1)}, bf16[32,8,128]{2,1,0:T(8,128)(2,1)S(1)}, u32[]{:S(2)}, u32[]{:S(2)}) collective-permute-start(bf16[32,8,128]{2,1,0:T(8,128)(2,1)S(1)} %get-tuple-element.725), channel_id=1, source_target_pairs={{0,2},{1,3},{4,6},{5,7},{8,10},{9,11},{12,14},{13,15},{16,18},{17,... | collective-permute-start | bytes 196616 | tf_op jit(solution)/shard_map/while/body/eval_jaxpr/ppermute | solution.py:29
  197.9 1.9 all_gather.59
  199.8 1.9 all_gather.60
  203.2 4.6 %collective-permute-start.1 = (bf16[192,1,128]{2,1,0:T(2,128)(2,1)S(1)}, bf16[192,1,128]{2,1,0:T(2,128)(2,1)S(1)}, u32[]{:S(2)}, u32[]{:S(2)}) collective-permute-start(bf16[192,1,128]{2,1,0:T(2,128)(2,1)S(1)} %get-tuple-element.690), channel_id=1, source_target_pairs={{0,4},{4,8},{8,12},{1,5},{5,9},{9,13},{2,6},{6,10},{10,14},{3,7},{... | collective-permute-start | bytes 147464 | tf_op jit(solution)/shard_map/while/body/eval_jaxpr/ppermute | solution.py:16
  210.1 4.1 %select_maximum_fusion.6 = bf16[192,10,130]{2,1,0:T(8,128)(2,1)S(1)} fusion(bf16[192,1,128]{2,1,0:T(2,128)(2,1)S(1)} %collective-permute-done, bf16[192,1,128]{2,1,0:T(2,128)(2,1)S(1)} %collective-permute-done.1, bf16[64,8,128]{2,1,0:T(8,128)(2,1)S(1)} %all_gather.59, bf16[64,8,128]{2,1,0:T(8,128)(2,1)S(1)} %all_gather.60, ...), kind=kLoop, calls=%fused_computation.5.clone.1 | loop fusion | flops 4492800 | bytes 990720 | tf_op jit(solution)/shard_map/while/body/eval_jaxpr/concatenate | solution.py:18
  217.3 1.9 all_gather.61
  220.6 5.0 %collective-permute-start.3 = (bf16[64,1,128]{2,1,0:T(2,128)(2,1)S(1)}, bf16[64,1,128]{2,1,0:T(2,128)(2,1)S(1)}, u32[]{:S(2)}, u32[]{:S(2)}) collective-permute-start(bf16[64,1,128]{2,1,0:T(2,128)(2,1)S(1)} %get-tuple-element.700), channel_id=1, source_target_pairs={{0,4},{4,8},{8,12},{1,5},{5,9},{9,13},{2,6},{6,10},{10,14},{3,7},{... | collective-permute-start | bytes 49160 | tf_op jit(solution)/shard_map/while/body/eval_jaxpr/ppermute | solution.py:16
  229.6 1.9 all_gather.62
  232.9 4.9 %collective-permute-start.5 = (bf16[64,1,128]{2,1,0:T(2,128)(2,1)S(1)}, bf16[64,1,128]{2,1,0:T(2,128)(2,1)S(1)}, u32[]{:S(2)}, u32[]{:S(2)}) collective-permute-start(bf16[64,1,128]{2,1,0:T(2,128)(2,1)S(1)} %get-tuple-element.710), channel_id=1, source_target_pairs={{0,4},{4,8},{8,12},{1,5},{5,9},{9,13},{2,6},{6,10},{10,14},{3,7},{... | collective-permute-start | bytes 49160 | tf_op jit(solution)/shard_map/while/body/eval_jaxpr/ppermute | solution.py:16
  243.3 4.6 %collective-permute-start.7 = (bf16[32,8,128]{2,1,0:T(8,128)(2,1)S(1)}, bf16[32,8,128]{2,1,0:T(8,128)(2,1)S(1)}, u32[]{:S(2)}, u32[]{:S(2)}) collective-permute-start(bf16[32,8,128]{2,1,0:T(8,128)(2,1)S(1)} %fusion.295), channel_id=1, source_target_pairs={{0,4},{4,8},{8,12},{1,5},{5,9},{9,13},{2,6},{6,10},{10,14},{3,7},{... | collective-permute-start | bytes 196616 | tf_op jit(solution)/shard_map/while/body/eval_jaxpr/ppermute | solution.py:16
  253.4 4.3 %collective-permute-start.8 = (bf16[32,8,128]{2,1,0:T(8,128)(2,1)S(1)}, bf16[32,8,128]{2,1,0:T(8,128)(2,1)S(1)}, u32[]{:S(2)}, u32[]{:S(2)}) collective-permute-start(bf16[32,8,128]{2,1,0:T(8,128)(2,1)S(1)} %get-tuple-element.725), channel_id=1, source_target_pairs={{0,2},{1,3},{4,6},{5,7},{8,10},{9,11},{12,14},{13,15},{16,18},{17,... | collective-permute-start | bytes 196616 | tf_op jit(solution)/shard_map/while/body/eval_jaxpr/ppermute | solution.py:29
  267.6 4.6 %collective-permute-start.1 = (bf16[192,1,128]{2,1,0:T(2,128)(2,1)S(1)}, bf16[192,1,128]{2,1,0:T(2,128)(2,1)S(1)}, u32[]{:S(2)}, u32[]{:S(2)}) collective-permute-start(bf16[192,1,128]{2,1,0:T(2,128)(2,1)S(1)} %get-tuple-element.690), channel_id=1, source_target_pairs={{0,4},{4,8},{8,12},{1,5},{5,9},{9,13},{2,6},{6,10},{10,14},{3,7},{... | collective-permute-start | bytes 147464 | tf_op jit(solution)/shard_map/while/body/eval_jaxpr/ppermute | solution.py:16
  274.5 4.1 %select_maximum_fusion.6 = bf16[192,10,130]{2,1,0:T(8,128)(2,1)S(1)} fusion(bf16[192,1,128]{2,1,0:T(2,128)(2,1)S(1)} %collective-permute-done, bf16[192,1,128]{2,1,0:T(2,128)(2,1)S(1)} %collective-permute-done.1, bf16[64,8,128]{2,1,0:T(8,128)(2,1)S(1)} %all_gather.59, bf16[64,8,128]{2,1,0:T(8,128)(2,1)S(1)} %all_gather.60, ...), kind=kLoop, calls=%fused_computation.5.clone.1 | loop fusion | flops 4492800 | bytes 990720 | tf_op jit(solution)/shard_map/while/body/eval_jaxpr/concatenate | solution.py:18
  281.7 1.9 all_gather.61
  285.0 5.0 %collective-permute-start.3 = (bf16[64,1,128]{2,1,0:T(2,128)(2,1)S(1)}, bf16[64,1,128]{2,1,0:T(2,128)(2,1)S(1)}, u32[]{:S(2)}, u32[]{:S(2)}) collective-permute-start(bf16[64,1,128]{2,1,0:T(2,128)(2,1)S(1)} %get-tuple-element.700), channel_id=1, source_target_pairs={{0,4},{4,8},{8,12},{1,5},{5,9},{9,13},{2,6},{6,10},{10,14},{3,7},{... | collective-permute-start | bytes 49160 | tf_op jit(solution)/shard_map/while/body/eval_jaxpr/ppermute | solution.py:16
  294.0 1.9 all_gather.62
  297.3 4.9 %collective-permute-start.5 = (bf16[64,1,128]{2,1,0:T(2,128)(2,1)S(1)}, bf16[64,1,128]{2,1,0:T(2,128)(2,1)S(1)}, u32[]{:S(2)}, u32[]{:S(2)}) collective-permute-start(bf16[64,1,128]{2,1,0:T(2,128)(2,1)S(1)} %get-tuple-element.710), channel_id=1, source_target_pairs={{0,4},{4,8},{8,12},{1,5},{5,9},{9,13},{2,6},{6,10},{10,14},{3,7},{... | collective-permute-start | bytes 49160 | tf_op jit(solution)/shard_map/while/body/eval_jaxpr/ppermute | solution.py:16
  307.7 4.6 %collective-permute-start.7 = (bf16[32,8,128]{2,1,0:T(8,128)(2,1)S(1)}, bf16[32,8,128]{2,1,0:T(8,128)(2,1)S(1)}, u32[]{:S(2)}, u32[]{:S(2)}) collective-permute-start(bf16[32,8,128]{2,1,0:T(8,128)(2,1)S(1)} %fusion.295), channel_id=1, source_target_pairs={{0,4},{4,8},{8,12},{1,5},{5,9},{9,13},{2,6},{6,10},{10,14},{3,7},{... | collective-permute-start | bytes 196616 | tf_op jit(solution)/shard_map/while/body/eval_jaxpr/ppermute | solution.py:16
  317.8 4.3 %collective-permute-start.8 = (bf16[32,8,128]{2,1,0:T(8,128)(2,1)S(1)}, bf16[32,8,128]{2,1,0:T(8,128)(2,1)S(1)}, u32[]{:S(2)}, u32[]{:S(2)}) collective-permute-start(bf16[32,8,128]{2,1,0:T(8,128)(2,1)S(1)} %get-tuple-element.725), channel_id=1, source_target_pairs={{0,2},{1,3},{4,6},{5,7},{8,10},{9,11},{12,14},{13,15},{16,18},{17,... | collective-permute-start | bytes 196616 | tf_op jit(solution)/shard_map/while/body/eval_jaxpr/ppermute | solution.py:29
  (416 shorter events, 127.9 us)
Async XLA Ops:
  8.5 7.9 %collective-permute-start = (bf16[192,1,128]{2,1,0:T(2,128)(2,1)S(1)}, bf16[192,1,128]{2,1,0:T(2,128)(2,1)S(1)}, u32[]{:S(2)}, u32[]{:S(2)}) collective-permute-start(bf16[192,1,128]{2,1,0:T(2,128)(2,1)S(1)} %get-tuple-element.689), channel_id=1, source_target_pairs={{4,0},{8,4},{12,8},{5,1},{9,5},{13,9},{6,2},{10,6},{14,10},{7,3},{... | collective-permute-start | bytes 147464 | tf_op jit(solution)/shard_map/while/body/eval_jaxpr/ppermute | solution.py:17
  9.8 7.8 %collective-permute-start.1 = (bf16[192,1,128]{2,1,0:T(2,128)(2,1)S(1)}, bf16[192,1,128]{2,1,0:T(2,128)(2,1)S(1)}, u32[]{:S(2)}, u32[]{:S(2)}) collective-permute-start(bf16[192,1,128]{2,1,0:T(2,128)(2,1)S(1)} %get-tuple-element.690), channel_id=1, source_target_pairs={{0,4},{4,8},{8,12},{1,5},{5,9},{9,13},{2,6},{6,10},{10,14},{3,7},{... | collective-permute-start | bytes 147464 | tf_op jit(solution)/shard_map/while/body/eval_jaxpr/ppermute | solution.py:16
  26.8 6.3 %collective-permute-start.2 = (bf16[64,1,128]{2,1,0:T(2,128)(2,1)S(1)}, bf16[64,1,128]{2,1,0:T(2,128)(2,1)S(1)}, u32[]{:S(2)}, u32[]{:S(2)}) collective-permute-start(bf16[64,1,128]{2,1,0:T(2,128)(2,1)S(1)} %get-tuple-element.699), channel_id=1, source_target_pairs={{4,0},{8,4},{12,8},{5,1},{9,5},{13,9},{6,2},{10,6},{14,10},{7,3},{... | collective-permute-start | bytes 49160 | tf_op jit(solution)/shard_map/while/body/eval_jaxpr/ppermute | solution.py:17
  28.1 6.6 %collective-permute-start.3 = (bf16[64,1,128]{2,1,0:T(2,128)(2,1)S(1)}, bf16[64,1,128]{2,1,0:T(2,128)(2,1)S(1)}, u32[]{:S(2)}, u32[]{:S(2)}) collective-permute-start(bf16[64,1,128]{2,1,0:T(2,128)(2,1)S(1)} %get-tuple-element.700), channel_id=1, source_target_pairs={{0,4},{4,8},{8,12},{1,5},{5,9},{9,13},{2,6},{6,10},{10,14},{3,7},{... | collective-permute-start | bytes 49160 | tf_op jit(solution)/shard_map/while/body/eval_jaxpr/ppermute | solution.py:16
  39.1 7.9 %collective-permute-start.4 = (bf16[64,1,128]{2,1,0:T(2,128)(2,1)S(1)}, bf16[64,1,128]{2,1,0:T(2,128)(2,1)S(1)}, u32[]{:S(2)}, u32[]{:S(2)}) collective-permute-start(bf16[64,1,128]{2,1,0:T(2,128)(2,1)S(1)} %get-tuple-element.709), channel_id=1, source_target_pairs={{4,0},{8,4},{12,8},{5,1},{9,5},{13,9},{6,2},{10,6},{14,10},{7,3},{... | collective-permute-start | bytes 49160 | tf_op jit(solution)/shard_map/while/body/eval_jaxpr/ppermute | solution.py:17
  40.4 6.6 %collective-permute-start.5 = (bf16[64,1,128]{2,1,0:T(2,128)(2,1)S(1)}, bf16[64,1,128]{2,1,0:T(2,128)(2,1)S(1)}, u32[]{:S(2)}, u32[]{:S(2)}) collective-permute-start(bf16[64,1,128]{2,1,0:T(2,128)(2,1)S(1)} %get-tuple-element.710), channel_id=1, source_target_pairs={{0,4},{4,8},{8,12},{1,5},{5,9},{9,13},{2,6},{6,10},{10,14},{3,7},{... | collective-permute-start | bytes 49160 | tf_op jit(solution)/shard_map/while/body/eval_jaxpr/ppermute | solution.py:16
  49.5 10.3 %collective-permute-start.6 = (bf16[32,8,128]{2,1,0:T(8,128)(2,1)S(1)}, bf16[32,8,128]{2,1,0:T(8,128)(2,1)S(1)}, u32[]{:S(2)}, u32[]{:S(2)}) collective-permute-start(bf16[32,8,128]{2,1,0:T(8,128)(2,1)S(1)} %fusion.295), channel_id=1, source_target_pairs={{4,0},{8,4},{12,8},{5,1},{9,5},{13,9},{6,2},{10,6},{14,10},{7,3},{... | collective-permute-start | bytes 196616 | tf_op jit(solution)/shard_map/while/body/eval_jaxpr/ppermute | solution.py:17
  50.8 9.1 %collective-permute-start.7 = (bf16[32,8,128]{2,1,0:T(8,128)(2,1)S(1)}, bf16[32,8,128]{2,1,0:T(8,128)(2,1)S(1)}, u32[]{:S(2)}, u32[]{:S(2)}) collective-permute-start(bf16[32,8,128]{2,1,0:T(8,128)(2,1)S(1)} %fusion.295), channel_id=1, source_target_pairs={{0,4},{4,8},{8,12},{1,5},{5,9},{9,13},{2,6},{6,10},{10,14},{3,7},{... | collective-permute-start | bytes 196616 | tf_op jit(solution)/shard_map/while/body/eval_jaxpr/ppermute | solution.py:16
  60.9 5.5 %collective-permute-start.8 = (bf16[32,8,128]{2,1,0:T(8,128)(2,1)S(1)}, bf16[32,8,128]{2,1,0:T(8,128)(2,1)S(1)}, u32[]{:S(2)}, u32[]{:S(2)}) collective-permute-start(bf16[32,8,128]{2,1,0:T(8,128)(2,1)S(1)} %get-tuple-element.725), channel_id=1, source_target_pairs={{0,2},{1,3},{4,6},{5,7},{8,10},{9,11},{12,14},{13,15},{16,18},{17,... | collective-permute-start | bytes 196616 | tf_op jit(solution)/shard_map/while/body/eval_jaxpr/ppermute | solution.py:29
  73.1 7.0 %collective-permute-start = (bf16[192,1,128]{2,1,0:T(2,128)(2,1)S(1)}, bf16[192,1,128]{2,1,0:T(2,128)(2,1)S(1)}, u32[]{:S(2)}, u32[]{:S(2)}) collective-permute-start(bf16[192,1,128]{2,1,0:T(2,128)(2,1)S(1)} %get-tuple-element.689), channel_id=1, source_target_pairs={{4,0},{8,4},{12,8},{5,1},{9,5},{13,9},{6,2},{10,6},{14,10},{7,3},{... | collective-permute-start | bytes 147464 | tf_op jit(solution)/shard_map/while/body/eval_jaxpr/ppermute | solution.py:17
  74.4 6.9 %collective-permute-start.1 = (bf16[192,1,128]{2,1,0:T(2,128)(2,1)S(1)}, bf16[192,1,128]{2,1,0:T(2,128)(2,1)S(1)}, u32[]{:S(2)}, u32[]{:S(2)}) collective-permute-start(bf16[192,1,128]{2,1,0:T(2,128)(2,1)S(1)} %get-tuple-element.690), channel_id=1, source_target_pairs={{0,4},{4,8},{8,12},{1,5},{5,9},{9,13},{2,6},{6,10},{10,14},{3,7},{... | collective-permute-start | bytes 147464 | tf_op jit(solution)/shard_map/while/body/eval_jaxpr/ppermute | solution.py:16
  90.5 6.3 %collective-permute-start.2 = (bf16[64,1,128]{2,1,0:T(2,128)(2,1)S(1)}, bf16[64,1,128]{2,1,0:T(2,128)(2,1)S(1)}, u32[]{:S(2)}, u32[]{:S(2)}) collective-permute-start(bf16[64,1,128]{2,1,0:T(2,128)(2,1)S(1)} %get-tuple-element.699), channel_id=1, source_target_pairs={{4,0},{8,4},{12,8},{5,1},{9,5},{13,9},{6,2},{10,6},{14,10},{7,3},{... | collective-permute-start | bytes 49160 | tf_op jit(solution)/shard_map/while/body/eval_jaxpr/ppermute | solution.py:17
  91.8 6.6 %collective-permute-start.3 = (bf16[64,1,128]{2,1,0:T(2,128)(2,1)S(1)}, bf16[64,1,128]{2,1,0:T(2,128)(2,1)S(1)}, u32[]{:S(2)}, u32[]{:S(2)}) collective-permute-start(bf16[64,1,128]{2,1,0:T(2,128)(2,1)S(1)} %get-tuple-element.700), channel_id=1, source_target_pairs={{0,4},{4,8},{8,12},{1,5},{5,9},{9,13},{2,6},{6,10},{10,14},{3,7},{... | collective-permute-start | bytes 49160 | tf_op jit(solution)/shard_map/while/body/eval_jaxpr/ppermute | solution.py:16
  102.8 7.9 %collective-permute-start.4 = (bf16[64,1,128]{2,1,0:T(2,128)(2,1)S(1)}, bf16[64,1,128]{2,1,0:T(2,128)(2,1)S(1)}, u32[]{:S(2)}, u32[]{:S(2)}) collective-permute-start(bf16[64,1,128]{2,1,0:T(2,128)(2,1)S(1)} %get-tuple-element.709), channel_id=1, source_target_pairs={{4,0},{8,4},{12,8},{5,1},{9,5},{13,9},{6,2},{10,6},{14,10},{7,3},{... | collective-permute-start | bytes 49160 | tf_op jit(solution)/shard_map/while/body/eval_jaxpr/ppermute | solution.py:17
  104.1 6.6 %collective-permute-start.5 = (bf16[64,1,128]{2,1,0:T(2,128)(2,1)S(1)}, bf16[64,1,128]{2,1,0:T(2,128)(2,1)S(1)}, u32[]{:S(2)}, u32[]{:S(2)}) collective-permute-start(bf16[64,1,128]{2,1,0:T(2,128)(2,1)S(1)} %get-tuple-element.710), channel_id=1, source_target_pairs={{0,4},{4,8},{8,12},{1,5},{5,9},{9,13},{2,6},{6,10},{10,14},{3,7},{... | collective-permute-start | bytes 49160 | tf_op jit(solution)/shard_map/while/body/eval_jaxpr/ppermute | solution.py:16
  113.2 10.3 %collective-permute-start.6 = (bf16[32,8,128]{2,1,0:T(8,128)(2,1)S(1)}, bf16[32,8,128]{2,1,0:T(8,128)(2,1)S(1)}, u32[]{:S(2)}, u32[]{:S(2)}) collective-permute-start(bf16[32,8,128]{2,1,0:T(8,128)(2,1)S(1)} %fusion.295), channel_id=1, source_target_pairs={{4,0},{8,4},{12,8},{5,1},{9,5},{13,9},{6,2},{10,6},{14,10},{7,3},{... | collective-permute-start | bytes 196616 | tf_op jit(solution)/shard_map/while/body/eval_jaxpr/ppermute | solution.py:17
  114.5 9.0 %collective-permute-start.7 = (bf16[32,8,128]{2,1,0:T(8,128)(2,1)S(1)}, bf16[32,8,128]{2,1,0:T(8,128)(2,1)S(1)}, u32[]{:S(2)}, u32[]{:S(2)}) collective-permute-start(bf16[32,8,128]{2,1,0:T(8,128)(2,1)S(1)} %fusion.295), channel_id=1, source_target_pairs={{0,4},{4,8},{8,12},{1,5},{5,9},{9,13},{2,6},{6,10},{10,14},{3,7},{... | collective-permute-start | bytes 196616 | tf_op jit(solution)/shard_map/while/body/eval_jaxpr/ppermute | solution.py:16
  124.0 5.1 %collective-permute-start.9 = (bf16[32,8,128]{2,1,0:T(8,128)(2,1)S(1)}, bf16[32,8,128]{2,1,0:T(8,128)(2,1)S(1)}, u32[]{:S(2)}, u32[]{:S(2)}) collective-permute-start(bf16[32,8,128]{2,1,0:T(8,128)(2,1)S(1)} %get-tuple-element.726), channel_id=1, source_target_pairs={} | collective-permute-start | bytes 196616 | tf_op jit(solution)/shard_map/while/body/eval_jaxpr/ppermute | solution.py:29
  124.6 6.2 %collective-permute-start.8 = (bf16[32,8,128]{2,1,0:T(8,128)(2,1)S(1)}, bf16[32,8,128]{2,1,0:T(8,128)(2,1)S(1)}, u32[]{:S(2)}, u32[]{:S(2)}) collective-permute-start(bf16[32,8,128]{2,1,0:T(8,128)(2,1)S(1)} %get-tuple-element.725), channel_id=1, source_target_pairs={{0,2},{1,3},{4,6},{5,7},{8,10},{9,11},{12,14},{13,15},{16,18},{17,... | collective-permute-start | bytes 196616 | tf_op jit(solution)/shard_map/while/body/eval_jaxpr/ppermute | solution.py:29
  137.5 7.0 %collective-permute-start = (bf16[192,1,128]{2,1,0:T(2,128)(2,1)S(1)}, bf16[192,1,128]{2,1,0:T(2,128)(2,1)S(1)}, u32[]{:S(2)}, u32[]{:S(2)}) collective-permute-start(bf16[192,1,128]{2,1,0:T(2,128)(2,1)S(1)} %get-tuple-element.689), channel_id=1, source_target_pairs={{4,0},{8,4},{12,8},{5,1},{9,5},{13,9},{6,2},{10,6},{14,10},{7,3},{... | collective-permute-start | bytes 147464 | tf_op jit(solution)/shard_map/while/body/eval_jaxpr/ppermute | solution.py:17
  138.8 6.9 %collective-permute-start.1 = (bf16[192,1,128]{2,1,0:T(2,128)(2,1)S(1)}, bf16[192,1,128]{2,1,0:T(2,128)(2,1)S(1)}, u32[]{:S(2)}, u32[]{:S(2)}) collective-permute-start(bf16[192,1,128]{2,1,0:T(2,128)(2,1)S(1)} %get-tuple-element.690), channel_id=1, source_target_pairs={{0,4},{4,8},{8,12},{1,5},{5,9},{9,13},{2,6},{6,10},{10,14},{3,7},{... | collective-permute-start | bytes 147464 | tf_op jit(solution)/shard_map/while/body/eval_jaxpr/ppermute | solution.py:16
  154.9 6.3 %collective-permute-start.2 = (bf16[64,1,128]{2,1,0:T(2,128)(2,1)S(1)}, bf16[64,1,128]{2,1,0:T(2,128)(2,1)S(1)}, u32[]{:S(2)}, u32[]{:S(2)}) collective-permute-start(bf16[64,1,128]{2,1,0:T(2,128)(2,1)S(1)} %get-tuple-element.699), channel_id=1, source_target_pairs={{4,0},{8,4},{12,8},{5,1},{9,5},{13,9},{6,2},{10,6},{14,10},{7,3},{... | collective-permute-start | bytes 49160 | tf_op jit(solution)/shard_map/while/body/eval_jaxpr/ppermute | solution.py:17
  156.2 6.6 %collective-permute-start.3 = (bf16[64,1,128]{2,1,0:T(2,128)(2,1)S(1)}, bf16[64,1,128]{2,1,0:T(2,128)(2,1)S(1)}, u32[]{:S(2)}, u32[]{:S(2)}) collective-permute-start(bf16[64,1,128]{2,1,0:T(2,128)(2,1)S(1)} %get-tuple-element.700), channel_id=1, source_target_pairs={{0,4},{4,8},{8,12},{1,5},{5,9},{9,13},{2,6},{6,10},{10,14},{3,7},{... | collective-permute-start | bytes 49160 | tf_op jit(solution)/shard_map/while/body/eval_jaxpr/ppermute | solution.py:16
  167.2 7.9 %collective-permute-start.4 = (bf16[64,1,128]{2,1,0:T(2,128)(2,1)S(1)}, bf16[64,1,128]{2,1,0:T(2,128)(2,1)S(1)}, u32[]{:S(2)}, u32[]{:S(2)}) collective-permute-start(bf16[64,1,128]{2,1,0:T(2,128)(2,1)S(1)} %get-tuple-element.709), channel_id=1, source_target_pairs={{4,0},{8,4},{12,8},{5,1},{9,5},{13,9},{6,2},{10,6},{14,10},{7,3},{... | collective-permute-start | bytes 49160 | tf_op jit(solution)/shard_map/while/body/eval_jaxpr/ppermute | solution.py:17
  168.5 6.6 %collective-permute-start.5 = (bf16[64,1,128]{2,1,0:T(2,128)(2,1)S(1)}, bf16[64,1,128]{2,1,0:T(2,128)(2,1)S(1)}, u32[]{:S(2)}, u32[]{:S(2)}) collective-permute-start(bf16[64,1,128]{2,1,0:T(2,128)(2,1)S(1)} %get-tuple-element.710), channel_id=1, source_target_pairs={{0,4},{4,8},{8,12},{1,5},{5,9},{9,13},{2,6},{6,10},{10,14},{3,7},{... | collective-permute-start | bytes 49160 | tf_op jit(solution)/shard_map/while/body/eval_jaxpr/ppermute | solution.py:16
  177.6 10.3 %collective-permute-start.6 = (bf16[32,8,128]{2,1,0:T(8,128)(2,1)S(1)}, bf16[32,8,128]{2,1,0:T(8,128)(2,1)S(1)}, u32[]{:S(2)}, u32[]{:S(2)}) collective-permute-start(bf16[32,8,128]{2,1,0:T(8,128)(2,1)S(1)} %fusion.295), channel_id=1, source_target_pairs={{4,0},{8,4},{12,8},{5,1},{9,5},{13,9},{6,2},{10,6},{14,10},{7,3},{... | collective-permute-start | bytes 196616 | tf_op jit(solution)/shard_map/while/body/eval_jaxpr/ppermute | solution.py:17
  178.9 9.0 %collective-permute-start.7 = (bf16[32,8,128]{2,1,0:T(8,128)(2,1)S(1)}, bf16[32,8,128]{2,1,0:T(8,128)(2,1)S(1)}, u32[]{:S(2)}, u32[]{:S(2)}) collective-permute-start(bf16[32,8,128]{2,1,0:T(8,128)(2,1)S(1)} %fusion.295), channel_id=1, source_target_pairs={{0,4},{4,8},{8,12},{1,5},{5,9},{9,13},{2,6},{6,10},{10,14},{3,7},{... | collective-permute-start | bytes 196616 | tf_op jit(solution)/shard_map/while/body/eval_jaxpr/ppermute | solution.py:16
  188.3 5.1 %collective-permute-start.9 = (bf16[32,8,128]{2,1,0:T(8,128)(2,1)S(1)}, bf16[32,8,128]{2,1,0:T(8,128)(2,1)S(1)}, u32[]{:S(2)}, u32[]{:S(2)}) collective-permute-start(bf16[32,8,128]{2,1,0:T(8,128)(2,1)S(1)} %get-tuple-element.726), channel_id=1, source_target_pairs={} | collective-permute-start | bytes 196616 | tf_op jit(solution)/shard_map/while/body/eval_jaxpr/ppermute | solution.py:29
  189.0 6.2 %collective-permute-start.8 = (bf16[32,8,128]{2,1,0:T(8,128)(2,1)S(1)}, bf16[32,8,128]{2,1,0:T(8,128)(2,1)S(1)}, u32[]{:S(2)}, u32[]{:S(2)}) collective-permute-start(bf16[32,8,128]{2,1,0:T(8,128)(2,1)S(1)} %get-tuple-element.725), channel_id=1, source_target_pairs={{0,2},{1,3},{4,6},{5,7},{8,10},{9,11},{12,14},{13,15},{16,18},{17,... | collective-permute-start | bytes 196616 | tf_op jit(solution)/shard_map/while/body/eval_jaxpr/ppermute | solution.py:29
  201.9 7.0 %collective-permute-start = (bf16[192,1,128]{2,1,0:T(2,128)(2,1)S(1)}, bf16[192,1,128]{2,1,0:T(2,128)(2,1)S(1)}, u32[]{:S(2)}, u32[]{:S(2)}) collective-permute-start(bf16[192,1,128]{2,1,0:T(2,128)(2,1)S(1)} %get-tuple-element.689), channel_id=1, source_target_pairs={{4,0},{8,4},{12,8},{5,1},{9,5},{13,9},{6,2},{10,6},{14,10},{7,3},{... | collective-permute-start | bytes 147464 | tf_op jit(solution)/shard_map/while/body/eval_jaxpr/ppermute | solution.py:17
  203.2 6.9 %collective-permute-start.1 = (bf16[192,1,128]{2,1,0:T(2,128)(2,1)S(1)}, bf16[192,1,128]{2,1,0:T(2,128)(2,1)S(1)}, u32[]{:S(2)}, u32[]{:S(2)}) collective-permute-start(bf16[192,1,128]{2,1,0:T(2,128)(2,1)S(1)} %get-tuple-element.690), channel_id=1, source_target_pairs={{0,4},{4,8},{8,12},{1,5},{5,9},{9,13},{2,6},{6,10},{10,14},{3,7},{... | collective-permute-start | bytes 147464 | tf_op jit(solution)/shard_map/while/body/eval_jaxpr/ppermute | solution.py:16
  219.3 6.3 %collective-permute-start.2 = (bf16[64,1,128]{2,1,0:T(2,128)(2,1)S(1)}, bf16[64,1,128]{2,1,0:T(2,128)(2,1)S(1)}, u32[]{:S(2)}, u32[]{:S(2)}) collective-permute-start(bf16[64,1,128]{2,1,0:T(2,128)(2,1)S(1)} %get-tuple-element.699), channel_id=1, source_target_pairs={{4,0},{8,4},{12,8},{5,1},{9,5},{13,9},{6,2},{10,6},{14,10},{7,3},{... | collective-permute-start | bytes 49160 | tf_op jit(solution)/shard_map/while/body/eval_jaxpr/ppermute | solution.py:17
  220.6 6.6 %collective-permute-start.3 = (bf16[64,1,128]{2,1,0:T(2,128)(2,1)S(1)}, bf16[64,1,128]{2,1,0:T(2,128)(2,1)S(1)}, u32[]{:S(2)}, u32[]{:S(2)}) collective-permute-start(bf16[64,1,128]{2,1,0:T(2,128)(2,1)S(1)} %get-tuple-element.700), channel_id=1, source_target_pairs={{0,4},{4,8},{8,12},{1,5},{5,9},{9,13},{2,6},{6,10},{10,14},{3,7},{... | collective-permute-start | bytes 49160 | tf_op jit(solution)/shard_map/while/body/eval_jaxpr/ppermute | solution.py:16
  231.6 7.9 %collective-permute-start.4 = (bf16[64,1,128]{2,1,0:T(2,128)(2,1)S(1)}, bf16[64,1,128]{2,1,0:T(2,128)(2,1)S(1)}, u32[]{:S(2)}, u32[]{:S(2)}) collective-permute-start(bf16[64,1,128]{2,1,0:T(2,128)(2,1)S(1)} %get-tuple-element.709), channel_id=1, source_target_pairs={{4,0},{8,4},{12,8},{5,1},{9,5},{13,9},{6,2},{10,6},{14,10},{7,3},{... | collective-permute-start | bytes 49160 | tf_op jit(solution)/shard_map/while/body/eval_jaxpr/ppermute | solution.py:17
  232.9 6.6 %collective-permute-start.5 = (bf16[64,1,128]{2,1,0:T(2,128)(2,1)S(1)}, bf16[64,1,128]{2,1,0:T(2,128)(2,1)S(1)}, u32[]{:S(2)}, u32[]{:S(2)}) collective-permute-start(bf16[64,1,128]{2,1,0:T(2,128)(2,1)S(1)} %get-tuple-element.710), channel_id=1, source_target_pairs={{0,4},{4,8},{8,12},{1,5},{5,9},{9,13},{2,6},{6,10},{10,14},{3,7},{... | collective-permute-start | bytes 49160 | tf_op jit(solution)/shard_map/while/body/eval_jaxpr/ppermute | solution.py:16
  242.0 10.3 %collective-permute-start.6 = (bf16[32,8,128]{2,1,0:T(8,128)(2,1)S(1)}, bf16[32,8,128]{2,1,0:T(8,128)(2,1)S(1)}, u32[]{:S(2)}, u32[]{:S(2)}) collective-permute-start(bf16[32,8,128]{2,1,0:T(8,128)(2,1)S(1)} %fusion.295), channel_id=1, source_target_pairs={{4,0},{8,4},{12,8},{5,1},{9,5},{13,9},{6,2},{10,6},{14,10},{7,3},{... | collective-permute-start | bytes 196616 | tf_op jit(solution)/shard_map/while/body/eval_jaxpr/ppermute | solution.py:17
  243.3 9.1 %collective-permute-start.7 = (bf16[32,8,128]{2,1,0:T(8,128)(2,1)S(1)}, bf16[32,8,128]{2,1,0:T(8,128)(2,1)S(1)}, u32[]{:S(2)}, u32[]{:S(2)}) collective-permute-start(bf16[32,8,128]{2,1,0:T(8,128)(2,1)S(1)} %fusion.295), channel_id=1, source_target_pairs={{0,4},{4,8},{8,12},{1,5},{5,9},{9,13},{2,6},{6,10},{10,14},{3,7},{... | collective-permute-start | bytes 196616 | tf_op jit(solution)/shard_map/while/body/eval_jaxpr/ppermute | solution.py:16
  253.4 6.2 %collective-permute-start.8 = (bf16[32,8,128]{2,1,0:T(8,128)(2,1)S(1)}, bf16[32,8,128]{2,1,0:T(8,128)(2,1)S(1)}, u32[]{:S(2)}, u32[]{:S(2)}) collective-permute-start(bf16[32,8,128]{2,1,0:T(8,128)(2,1)S(1)} %get-tuple-element.725), channel_id=1, source_target_pairs={{0,2},{1,3},{4,6},{5,7},{8,10},{9,11},{12,14},{13,15},{16,18},{17,... | collective-permute-start | bytes 196616 | tf_op jit(solution)/shard_map/while/body/eval_jaxpr/ppermute | solution.py:29
  266.3 7.0 %collective-permute-start = (bf16[192,1,128]{2,1,0:T(2,128)(2,1)S(1)}, bf16[192,1,128]{2,1,0:T(2,128)(2,1)S(1)}, u32[]{:S(2)}, u32[]{:S(2)}) collective-permute-start(bf16[192,1,128]{2,1,0:T(2,128)(2,1)S(1)} %get-tuple-element.689), channel_id=1, source_target_pairs={{4,0},{8,4},{12,8},{5,1},{9,5},{13,9},{6,2},{10,6},{14,10},{7,3},{... | collective-permute-start | bytes 147464 | tf_op jit(solution)/shard_map/while/body/eval_jaxpr/ppermute | solution.py:17
  267.6 6.9 %collective-permute-start.1 = (bf16[192,1,128]{2,1,0:T(2,128)(2,1)S(1)}, bf16[192,1,128]{2,1,0:T(2,128)(2,1)S(1)}, u32[]{:S(2)}, u32[]{:S(2)}) collective-permute-start(bf16[192,1,128]{2,1,0:T(2,128)(2,1)S(1)} %get-tuple-element.690), channel_id=1, source_target_pairs={{0,4},{4,8},{8,12},{1,5},{5,9},{9,13},{2,6},{6,10},{10,14},{3,7},{... | collective-permute-start | bytes 147464 | tf_op jit(solution)/shard_map/while/body/eval_jaxpr/ppermute | solution.py:16
  283.7 6.3 %collective-permute-start.2 = (bf16[64,1,128]{2,1,0:T(2,128)(2,1)S(1)}, bf16[64,1,128]{2,1,0:T(2,128)(2,1)S(1)}, u32[]{:S(2)}, u32[]{:S(2)}) collective-permute-start(bf16[64,1,128]{2,1,0:T(2,128)(2,1)S(1)} %get-tuple-element.699), channel_id=1, source_target_pairs={{4,0},{8,4},{12,8},{5,1},{9,5},{13,9},{6,2},{10,6},{14,10},{7,3},{... | collective-permute-start | bytes 49160 | tf_op jit(solution)/shard_map/while/body/eval_jaxpr/ppermute | solution.py:17
  285.0 6.6 %collective-permute-start.3 = (bf16[64,1,128]{2,1,0:T(2,128)(2,1)S(1)}, bf16[64,1,128]{2,1,0:T(2,128)(2,1)S(1)}, u32[]{:S(2)}, u32[]{:S(2)}) collective-permute-start(bf16[64,1,128]{2,1,0:T(2,128)(2,1)S(1)} %get-tuple-element.700), channel_id=1, source_target_pairs={{0,4},{4,8},{8,12},{1,5},{5,9},{9,13},{2,6},{6,10},{10,14},{3,7},{... | collective-permute-start | bytes 49160 | tf_op jit(solution)/shard_map/while/body/eval_jaxpr/ppermute | solution.py:16
  296.0 7.9 %collective-permute-start.4 = (bf16[64,1,128]{2,1,0:T(2,128)(2,1)S(1)}, bf16[64,1,128]{2,1,0:T(2,128)(2,1)S(1)}, u32[]{:S(2)}, u32[]{:S(2)}) collective-permute-start(bf16[64,1,128]{2,1,0:T(2,128)(2,1)S(1)} %get-tuple-element.709), channel_id=1, source_target_pairs={{4,0},{8,4},{12,8},{5,1},{9,5},{13,9},{6,2},{10,6},{14,10},{7,3},{... | collective-permute-start | bytes 49160 | tf_op jit(solution)/shard_map/while/body/eval_jaxpr/ppermute | solution.py:17
  297.3 6.6 %collective-permute-start.5 = (bf16[64,1,128]{2,1,0:T(2,128)(2,1)S(1)}, bf16[64,1,128]{2,1,0:T(2,128)(2,1)S(1)}, u32[]{:S(2)}, u32[]{:S(2)}) collective-permute-start(bf16[64,1,128]{2,1,0:T(2,128)(2,1)S(1)} %get-tuple-element.710), channel_id=1, source_target_pairs={{0,4},{4,8},{8,12},{1,5},{5,9},{9,13},{2,6},{6,10},{10,14},{3,7},{... | collective-permute-start | bytes 49160 | tf_op jit(solution)/shard_map/while/body/eval_jaxpr/ppermute | solution.py:16
  306.4 10.3 %collective-permute-start.6 = (bf16[32,8,128]{2,1,0:T(8,128)(2,1)S(1)}, bf16[32,8,128]{2,1,0:T(8,128)(2,1)S(1)}, u32[]{:S(2)}, u32[]{:S(2)}) collective-permute-start(bf16[32,8,128]{2,1,0:T(8,128)(2,1)S(1)} %fusion.295), channel_id=1, source_target_pairs={{4,0},{8,4},{12,8},{5,1},{9,5},{13,9},{6,2},{10,6},{14,10},{7,3},{... | collective-permute-start | bytes 196616 | tf_op jit(solution)/shard_map/while/body/eval_jaxpr/ppermute | solution.py:17
  307.7 9.0 %collective-permute-start.7 = (bf16[32,8,128]{2,1,0:T(8,128)(2,1)S(1)}, bf16[32,8,128]{2,1,0:T(8,128)(2,1)S(1)}, u32[]{:S(2)}, u32[]{:S(2)}) collective-permute-start(bf16[32,8,128]{2,1,0:T(8,128)(2,1)S(1)} %fusion.295), channel_id=1, source_target_pairs={{0,4},{4,8},{8,12},{1,5},{5,9},{9,13},{2,6},{6,10},{10,14},{3,7},{... | collective-permute-start | bytes 196616 | tf_op jit(solution)/shard_map/while/body/eval_jaxpr/ppermute | solution.py:16
  317.1 5.1 %collective-permute-start.9 = (bf16[32,8,128]{2,1,0:T(8,128)(2,1)S(1)}, bf16[32,8,128]{2,1,0:T(8,128)(2,1)S(1)}, u32[]{:S(2)}, u32[]{:S(2)}) collective-permute-start(bf16[32,8,128]{2,1,0:T(8,128)(2,1)S(1)} %get-tuple-element.726), channel_id=1, source_target_pairs={} | collective-permute-start | bytes 196616 | tf_op jit(solution)/shard_map/while/body/eval_jaxpr/ppermute | solution.py:29
  317.8 6.2 %collective-permute-start.8 = (bf16[32,8,128]{2,1,0:T(8,128)(2,1)S(1)}, bf16[32,8,128]{2,1,0:T(8,128)(2,1)S(1)}, u32[]{:S(2)}, u32[]{:S(2)}) collective-permute-start(bf16[32,8,128]{2,1,0:T(8,128)(2,1)S(1)} %get-tuple-element.725), channel_id=1, source_target_pairs={{0,2},{1,3},{4,6},{5,7},{8,10},{9,11},{12,14},{13,15},{16,18},{17,... | collective-permute-start | bytes 196616 | tf_op jit(solution)/shard_map/while/body/eval_jaxpr/ppermute | solution.py:29
  (33 other events, 138.2 us)
where the time goes:
time: 327 us; the launch traced here: 325 us
  starting transfers between devices  146 us (45%)
  blocking collectives  47.5 us (15%)
  other arithmetic  32.7 us (10%)
  waiting for transfers between devices  28.1 us (9%)
  loops' own time  27 us (8%)
  local copies, waits for them, and re-layouts  22.6 us (7%)
  matrix products  20.8 us (6%)
    ppermute x20, starting transfers between devices, padded_2(): before = lax.ppermute(last, axis, up)  96.2 us
    concatenate x35, other arithmetic, padded_2(): array = jnp.concatenate([before, array, after], axis=dim)  30 us
    another operation x1, loops' own time, shards(): lax.fori_loop(0, segments + owners - 1, advance, initial)  27 us
    ppermute x20, starting transfers between devices, padded_2(): after = lax.ppermute(first, axis, down)  25.8 us
    ppermute x10, starting transfers between devices, shifted(): return lax.ppermute(block, axis, route)  24 us
    dot_general x135, matrix products, convolve_rows(): jnp.dot(weights[tap_index], window, preferred_element_type=jnp.float32)  20.8 us
    all_gather x10, blocking collectives, block_conv(): whole_input = lax.all_gather(own_part, 'chan', axis=0, tiled=True)  19 us
    ppermute x20, waiting for transfers between devices, padded_2(): before = lax.ppermute(last, axis, up)  13.7 us
  transfers between devices with their start and end apart: 50, of which 20 were waited for; matrix products, arithmetic and copies ran while one was open for 2% of the time, Pallas kernels for 0%

commit v1 on v0

v1 whole, which is shorter than its diff:
```python
import functools

import jax
import jax.numpy as jnp
from jax import lax
from jax.experimental import pallas as pl
from jax.experimental.pallas import tpu as pltpu
from jax.sharding import PartitionSpec as P

TAPS = 3
CHUNK = 8


def hop(array, axis, step):
    count = lax.axis_size(axis)
    if step % count == 0:
        return array
    return lax.ppermute(array, axis, [(i, (i + step) % count) for i in range(count)])


def moved(value, step):
    cols = value.shape[1]
    lane = lax.broadcasted_iota(jnp.int32, value.shape, 1)
    rolled = pltpu.roll(value, lax.rem(cols - step, cols), 1)
    return jnp.where((lane + step >= 0) & (lane + step < cols), rolled, 0.0)


def fan(value):
    taps = [moved(value, -1), value, moved(value, 1)]
    return [tap.astype(jnp.bfloat16) for tap in taps]


def recurrence(sizes, place, flows, w_join, w_first, w_second, b_join, b_first, b_second, *rest):
    frames, tiles, chans, groups, span, count, part, depth, cols = sizes
    n_blocks = frames * tiles * chans
    blocks, rest = rest[:n_blocks], rest[n_blocks:]
    outs, rest = rest[:groups], rest[groups:]
    slots, stage, features, sources, joined, history, arrived = rest
    channels = part * chans
    rows = tiles * depth
    tile, frame_here, chan = place[0], place[1], place[2]
    kept = history.shape[0]
    top = depth + 1

    def copies(segment, shift):
        for index in range(tiles * chans):
            yield pltpu.make_async_copy(
                blocks[shift * tiles * chans + index].at[segment],
                slots.at[shift % 2, index],
                arrived.at[shift % 2, index],
            )

    def load(segment):
        for copy in copies(segment, 0):
            copy.start()
        for shift in range(frames):
            if shift + 1 < frames:
                for copy in copies(segment, shift + 1):
                    copy.start()
            frame = lax.rem(frame_here - shift + frames, frames)
            pending = list(copies(segment, shift))
            for index in range(tiles * chans):
                source_tile = lax.rem(tile - index // chans + tiles, tiles)
                source_chan = lax.rem(chan - index % chans + chans, chans)
                pending[index].wait()
                block = slots[shift % 2, index, :part].astype(jnp.float32)
                stage[index] = block.reshape(part * depth, cols)
                first = pl.multiple_of(source_chan * part, part)
                for row in range(depth):
                    value = stage[index, pl.ds(row, part, stride=depth), :]
                    features[frame, source_tile * depth + row, pl.ds(first, part), :] = (
                        value.astype(jnp.bfloat16)
                    )

    def convolve(inputs, weights, bias, emit):
        def step(chunk, carried):
            above, here = carried
            start = chunk * CHUNK
            slabs = [
                jnp.concatenate([ref[start + row + 1] for ref in inputs], axis=0)
                for row in range(CHUNK)
            ]
            partial = jnp.dot(
                weights, jnp.concatenate(slabs, axis=1), preferred_element_type=jnp.float32
            )
            for row in range(CHUNK):
                one = partial[:, row * cols : (row + 1) * cols]
                emit(start + row, above + one[2 * channels :])
                above = here + one[channels : 2 * channels]
                here = bias + one[:channels]
            return above, here

        above, _ = lax.fori_loop(0, rows // CHUNK, step, (bias, bias))
        emit(rows, above)

    def spread(ref, slot, value):
        for tap, shifted in enumerate(fan(value)):
            ref[slot, tap * channels : (tap + 1) * channels, :] = shifted

    def displace(held, target, segment, field):
        def one_block(block, _):
            origin = lax.rem(tile - block + tiles, tiles)
            down = flows[segment, origin, field]
            right = flows[segment, origin, field + 1]
            for row in range(depth):
                at = block * depth + row
                value = held[top + at + down].astype(jnp.float32)
                spread(target, at + 1, moved(value, right))
            return 0

        lax.fori_loop(0, tiles, one_block, 0)

    for index in range(kept):
        history[index, :top] = jnp.zeros((top, channels, cols), jnp.bfloat16)
        history[index, top + rows :] = jnp.zeros((depth, channels, cols), jnp.bfloat16)

    for segment in range(count):
        load(segment)
        for frame in range(frames):
            inputs = [sources.at[0]]

            def spread_own(row, _, frame=frame):
                spread(sources.at[0], row + 1, features[frame, row].astype(jnp.float32))
                return 0

            lax.fori_loop(0, rows, spread_own, 0)
            for back, field in ((1, 2 * frame), (2, 2 * (frames + frame))):
                if frame >= back:
                    displace(history.at[(frame - back) % kept], sources.at[back], segment, field)
                    inputs.append(sources.at[back])
            width = TAPS * channels * len(inputs)
            new = history.at[frame % kept]

            def emit_join(slot, total):
                spread(joined, slot, jnp.where(total > 0, total, 0.1 * total))

            def emit_inner(slot, total):
                spread(sources.at[0], slot, jnp.maximum(total, 0.0))

            def emit_second(slot, total, new=new):
                state = joined[slot, channels : 2 * channels, :].astype(jnp.float32) + total
                new[top - 1 + slot] = state.astype(jnp.bfloat16)

            convolve(inputs, w_join[:, :width], b_join[...], emit_join)
            convolve([joined], w_first[...], b_first[...], emit_inner)
            convolve([sources.at[0]], w_second[...], b_second[...], emit_second)
            new[top - 1] = jnp.zeros((channels, cols), jnp.bfloat16)

            @pl.when(frame_here == frame)
            def _(segment=segment, new=new):
                first = pl.multiple_of(chan * part, part)
                for turn in range(groups):
                    target = lax.rem(tile + turn * span, tiles)
                    for row in range(depth):
                        value = new[top + target * depth + row, pl.ds(first, part), :]
                        stage[turn, pl.ds(row, part, stride=depth), :] = value.astype(jnp.float32)
                    whole = stage[turn].reshape(part, depth, cols)
                    outs[turn][segment] = whole.astype(jnp.bfloat16)


def shards(lr_feats, flow_prev, flow_second, w_join, b_join, w_first, b_first, w_second, b_second):
    segments, _, part, depth, cols = lr_feats.shape
    frames, tiles, chans = (lax.axis_size(name) for name in ("frames", "tiles", "chan"))
    tile, frame, chan = (lax.axis_index(name) for name in ("tiles", "frames", "chan"))
    span = max(1, tiles // segments)
    groups = tiles // span
    count = segments // groups
    channels = part * chans

    offsets = jnp.concatenate(
        [flow.reshape(segments, frames * 2) for flow in (flow_prev, flow_second)], axis=1
    )
    fields = offsets.shape[1]
    plane = jnp.pad(offsets.astype(jnp.bfloat16), ((0, 0), (0, cols - fields)))
    plane = jnp.broadcast_to(plane[:, None, None], (segments, 1, depth, cols))
    payload = jnp.concatenate([lr_feats[:, 0], plane], axis=1)

    def for_tile(index):
        return lax.dynamic_slice_in_dim(payload, lax.rem(index, tiles) // span * count, count, 0)

    own = [hop(for_tile(tile + shift), "tiles", shift) for shift in range(tiles)]
    blocks = []
    for turn in range(frames):
        for shift in range(tiles):
            block = hop(own[shift], "frames", turn)
            blocks += [hop(block, "chan", side) for side in range(chans)]
    flows = jnp.stack([block[:, part, 0, :fields] for block in own], axis=1).astype(jnp.int32)

    def gathered(array, dim):
        pieces = [hop(array, "chan", side) for side in range(chans)]
        if chans == 2:
            low = jnp.where(chan == 0, pieces[0], pieces[1])
            high = jnp.where(chan == 0, pieces[1], pieces[0])
            return jnp.concatenate([low, high], axis=dim)
        return lax.all_gather(array, "chan", axis=dim, tiled=True)

    w_all = gathered(jnp.concatenate([w_join, w_first[0], w_second[0]], axis=2), 1)
    b_all = gathered(jnp.stack([b_join, b_first[0], b_second[0]]), 1)

    def arranged(weights):
        inputs = weights.shape[2] // channels
        split = weights.reshape(TAPS, TAPS, channels, inputs, channels)
        return split.transpose(0, 2, 3, 1, 4).reshape(TAPS * channels, inputs * TAPS * channels)

    w_sizes = (w_join.shape[2], w_first.shape[3], w_second.shape[3])
    edges = (w_sizes[0], w_sizes[0] + w_sizes[1])
    weights = [arranged(part_w) for part_w in jnp.split(w_all, edges, axis=2)]
    biases = [jnp.broadcast_to(row[:, None], (channels, cols)) for row in b_all]

    rows = tiles * depth
    kept = min(frames, 3)
    sizes = (frames, tiles, chans, groups, span, count, part, depth, cols)
    vmem = pl.BlockSpec(memory_space=pltpu.VMEM)
    smem = pl.BlockSpec(memory_space=pltpu.SMEM)
    block_shape = (part + 1, depth, cols)
    wide = TAPS * channels
    outs = pl.pallas_call(
        functools.partial(recurrence, sizes),
        out_shape=[jax.ShapeDtypeStruct((count, part, depth, cols), jnp.bfloat16)] * groups,
        in_specs=[smem, smem] + [vmem] * 6 + [pl.BlockSpec(memory_space=pl.ANY)] * len(blocks),
        out_specs=[vmem] * groups,
        scratch_shapes=[
            pltpu.VMEM((2, tiles * chans) + block_shape, jnp.bfloat16),
            pltpu.VMEM((tiles * chans, part * depth, cols), jnp.float32),
            pltpu.VMEM((frames, rows, channels, cols), jnp.bfloat16),
            pltpu.VMEM((3, rows + 1, wide, cols), jnp.bfloat16),
            pltpu.VMEM((rows + 1, wide, cols), jnp.bfloat16),
            pltpu.VMEM((kept, rows + 2 * depth + 1, channels, cols), jnp.bfloat16),
            pltpu.SemaphoreType.DMA((2, tiles * chans)),
        ],
    )(jnp.stack([tile, frame, chan]).astype(jnp.int32), flows, *weights, *biases, *blocks)

    done = jnp.stack([hop(out, "tiles", turn * span) for turn, out in enumerate(outs)])
    turn_of = lax.rem(tile // span - jnp.arange(groups) + groups, groups)
    return jnp.take(done, turn_of, axis=0).reshape(segments, 1, part, depth, cols)


def solution(mesh):
    in_specs = (
        P("clips", "frames", "chan", "tiles", None),
        P("clips", None, "tiles", None),
        P("clips", None, "tiles", None),
        P(None, "chan", None),
        P("chan"),
        P(None, None, "chan", None),
        P(None, "chan"),
        P(None, None, "chan", None),
        P(None, "chan"),
    )
    out_specs = P("clips", "frames", "chan", "tiles", None)
    return jax.shard_map(shards, mesh=mesh, in_specs=in_specs, out_specs=out_specs, check_vma=False)
```

time: 327 us -> 64.9 us (0.20)
  starting transfers between devices: 146 us -> 13 us
  blocking collectives: 47.5 us -> 0 us
  other arithmetic: 32.7 us -> 4.74 us
  loops' own time: 27 us -> 0 us
  matrix products: 20.8 us -> 0 us
  Pallas kernels: 0 us -> 18.3 us
  local copies, waits for them, and re-layouts: 22.6 us -> 9.24 us
  waiting for transfers between devices: 28.1 us -> 18.9 us
    ppermute x50 -> x20, starting transfers between devices: 146 us -> 13 us  [hop(): lax.ppermute(array, axis, [(i, (i + step) % count) for i in range(count)])]
    all_gather x25 -> x0, blocking collectives: 47.5 us -> none  [the longest x10 19 us: block_conv(): whole_input = lax.all_gather(own_part, 'chan', axis=0, tiled=True)]
    concatenate x40 -> x6, other arithmetic: 30.2 us -> 1.65 us  [the longest x1 1.03 us: shards(): payload = jnp.concatenate([lr_feats[:, 0], plane], axis=1)]
    another operation x1 -> x0, loops' own time: 27 us -> none  [shards(): lax.fori_loop(0, segments + owners - 1, advance, initial)]
    dot_general x135 -> x0, matrix products: 20.8 us -> none  [convolve_rows(): jnp.dot(weights[tap_index], window, preferred_element_type=jnp.float32)]
    pallas_call x0 -> x1, Pallas kernels: none -> 18.3 us  [shards(): pl.pallas_call(functools.partial(recurrence, sizes), out_shape=[jax.Shape...]
    slice x40 -> x0, local copies, waits for them, and re-layouts: 14.2 us -> none  [the longest x15 6.92 us: convolve_rows(): padded[:, tap_row:tap_row + row_count, tap_col:tap_col + col_count]]
    ppermute x50 -> x20, waiting for transfers between devices: 28.1 us -> 18.9 us  [hop(): lax.ppermute(array, axis, [(i, (i + step) % count) for i in range(count)])]
  transfers between devices with their start and end apart: 50 -> 20, of which waited for: 20 -> 7; matrix products, arithmetic and copies ran while one was open for 2% -> 10% of each run, Pallas kernels for 0% -> 0%
where the time goes in v1:
time: 64.9 us; the launch traced here: 64.6 us
  waiting for transfers between devices  18.9 us (29%)
  Pallas kernels  18.3 us (28%)
  starting transfers between devices  13 us (20%)
  local copies, waits for them, and re-layouts  9.24 us (14%)
  other arithmetic  4.74 us (7%)
    ppermute x20, waiting for transfers between devices, hop(): lax.ppermute(array, axis, [(i, (i + step) % count) for i in range(count)])  18.9 us
    pallas_call x1, Pallas kernels, shards(): pl.pallas_call(functools.partial(recurrence, sizes), out_shape=[jax.Shape...  18.3 us
    ppermute x20, starting transfers between devices, hop(): lax.ppermute(array, axis, [(i, (i + step) % count) for i in range(count)])  13 us
    reshape x3, local copies, waits for them, and re-layouts, arranged(): split.transpose(0, 2, 3, 1, 4)  2.71 us
    broadcast_in_dim x4, local copies, waits for them, and re-layouts, shards(): biases = [jnp.broadcast_to(row[:, None], (channels, cols)) for row in b_all]  2.05 us
    unnamed x47, local copies, waits for them, and re-layouts  1.87 us
  transfers between devices with their start and end apart: 20, of which 7 were waited for; matrix products, arithmetic and copies ran while one was open for 10% of the time, Pallas kernels for 0%

profile of v1, /device:TPU:0, one launch (start us, length us, event | category | flops | bytes accessed | tf_op | source)
XLA Modules:
  0.0 64.6 jit_solution(12813998648581821184)
XLA Ops:
  0.0 0.7 %copy-done.21 = s32[4,2,1,2]{0,3,2,1:T(2,128)S(1)} copy-done((s32[4,2,1,2]{0,3,2,1:T(2,128)S(1)}, s32[4,2,1,2]{0,3,2,1:T(2,128)}, u32[]{:S(2)}) %copy-start.21) | copy-done | bytes 88
  0.7 0.1 copy.32
  0.9 1.0 %fusion.4 = (bf16[1,33,8,128]{3,2,1,0:T(8,128)(2,1)S(1)}, bf16[1,33,8,128]{3,2,1,0:T(8,128)(2,1)S(1)}, bf16[1,33,8,128]{3,2,1,0:T(8,128)(2,1)S(1)}, bf16[1,33,8,128]{3,2,1,0:T(8,128)(2,1)S(1)}) fusion(s32[]{:T(128)S(6)} %select_n.72, bf16[4,1,8,128]{3,2,1,0:T(8,128)(2,1)S(1)} %broadcast_in_dim.38, bf16[4,32,8,128]{3,2,1,0:T(8,128)(2,1)} %bitcast.53, ...), kind=kLoop, calls=%fused_computation.23 | loop fusion | flops 135168 | bytes 540688 | tf_op jit(solution)/shard_map/concatenate | solution.py:176
  1.9 0.6 collective-permute-start.5
  2.5 2.6 %collective-permute-start.9 = (bf16[1,33,8,128]{3,2,1,0:T(8,128)(2,1)S(1)}, bf16[1,33,8,128]{3,2,1,0:T(8,128)(2,1)S(1)}, u32[]{:S(2)}, u32[]{:S(2)}) collective-permute-start(bf16[1,33,8,128]{3,2,1,0:T(8,128)(2,1)S(1)} %get-tuple-element.17.rest_0_), channel_id=1, source_target_pairs={{0,2},{2,0},{1,3},{3,1},{4,6},{6,4},{5,7},{7,5},{8,10},{10,8},{9,1... | collective-permute-start | bytes 202760 | tf_op jit(solution)/shard_map/ppermute | solution.py:18
  5.0 3.6 %collective-permute-start.2 = (bf16[1,33,8,128]{3,2,1,0:T(8,128)(2,1)S(1)}, bf16[1,33,8,128]{3,2,1,0:T(8,128)(2,1)S(1)}, u32[]{:S(2)}, u32[]{:S(2)}) collective-permute-start(bf16[1,33,8,128]{3,2,1,0:T(8,128)(2,1)S(1)} %get-tuple-element.20), channel_id=1, source_target_pairs={{0,12},{4,0},{8,4},{12,8},{1,13},{5,1},{9,5},{13,9},{2,14},{6,2},{... | collective-permute-start | bytes 202760 | tf_op jit(solution)/shard_map/ppermute | solution.py:18
  8.6 0.1 pad_maximum_fusion
  8.8 0.1 collective-permute-start.3
  8.9 0.5 copy-done.18
  9.5 0.1 collective-permute-start.4
  9.6 0.7 %pad_add_fusion.place = s32[3]{0:T(128)} fusion(s32[1]{0:T(128)} %bitcast.2, s32[1]{0:T(128)} %bitcast.1, s32[1]{0:T(128)} %bitcast), kind=kLoop, calls=%fused_computation.47 | loop fusion | flops 6 | bytes 24 | tf_op jit(solution)/shard_map/stack | solution.py:231
  10.3 0.4 copy.24
  10.7 0.1 pad_maximum_fusion.4
  10.8 6.2 %collective-permute-done.rest_2_ = bf16[1,33,8,128]{3,2,1,0:T(8,128)(2,1)S(1)} collective-permute-done((bf16[1,33,8,128]{3,2,1,0:T(8,128)(2,1)S(1)}, bf16[1,33,8,128]{3,2,1,0:T(8,128)(2,1)S(1)}, u32[]{:S(2)}, u32[]{:S(2)}) %collective-permute-start) | collective-permute-done | bytes 67616 | tf_op jit(solution)/shard_map/ppermute | solution.py:18
  17.0 5.2 %collective-permute-done.1.rest_4_ = bf16[1,33,8,128]{3,2,1,0:T(8,128)(2,1)S(1)} collective-permute-done((bf16[1,33,8,128]{3,2,1,0:T(8,128)(2,1)S(1)}, bf16[1,33,8,128]{3,2,1,0:T(8,128)(2,1)S(1)}, u32[]{:S(2)}, u32[]{:S(2)}) %collective-permute-start.1) | collective-permute-done | bytes 67616 | tf_op jit(solution)/shard_map/ppermute | solution.py:18
  22.2 0.5 collective-permute-start.7
  22.7 0.6 maximum_convert_fusion.flows
  23.3 0.5 collective-permute-start.11
  23.8 0.4 copy.25
  24.2 0.1 broadcast_select_fusion
  24.4 1.6 %collective-permute-start.13 = (bf16[1,33,8,128]{3,2,1,0:T(8,128)(2,1)S(1)}, bf16[1,33,8,128]{3,2,1,0:T(8,128)(2,1)S(1)}, u32[]{:S(2)}, u32[]{:S(2)}) collective-permute-start(bf16[1,33,8,128]{3,2,1,0:T(8,128)(2,1)S(1)} %collective-permute-done.1.rest_4_), channel_id=1, source_target_pairs={{0,2},{2,0},{1,3},{3,1},{4,6},{6,4},{5,7},{7,5},{8,10},{10,8},{9,1... | collective-permute-start | bytes 202760 | tf_op jit(solution)/shard_map/ppermute | solution.py:18
  25.9 0.5 collective-permute-start.15
  26.5 0.2 fusion
  26.7 0.9 %copy.28 = bf16[3,64,3,3,64]{4,3,2,1,0:T(4,128)(2,1)S(1)} copy(bf16[3,64,3,3,64]{1,4,2,3,0:T(8,128)(2,1)S(1)} %bitcast.48) | data formatting | bytes 442368 | tf_op jit(solution)/shard_map/transpose | solution.py:203
  27.7 1.1 %reshape.153.w_join = bf16[192,576]{1,0:T(8,128)(2,1)} reshape(bf16[3,64,3,3,64]{4,3,2,1,0:T(4,128)(2,1)S(1)} %copy.28) | data formatting | bytes 442368 | tf_op jit(solution)/shard_map/reshape | solution.py:203
  28.8 0.1 collective-permute-start.8
  28.9 0.5 collective-permute-start.10
  29.4 0.1 collective-permute-start.12
  29.5 0.2 collective-permute-done.13.rest_12_
  29.7 0.2 collective-permute-start.14
  29.9 0.5 collective-permute-done.15.rest_14_
  30.4 0.2 pad_maximum_fusion.1
  30.6 0.4 copy-done.12
  31.1 0.2 copy.29
  31.2 0.8 %reshape.155.w_first = bf16[192,192]{1,0:T(8,128)(2,1)} reshape(bf16[3,64,1,3,64]{4,3,1,0,2:T(4,128)(2,1)S(1)} %bitcast.49) | data formatting | bytes 147456 | tf_op jit(solution)/shard_map/reshape | solution.py:203
  32.0 0.2 copy.30
  32.2 0.8 %reshape.157.w_second = bf16[192,192]{1,0:T(8,128)(2,1)} reshape(bf16[3,64,1,3,64]{4,3,1,0,2:T(4,128)(2,1)S(1)} %bitcast.50) | data formatting | bytes 147456 | tf_op jit(solution)/shard_map/reshape | solution.py:203
  33.1 0.7 %broadcast_in_dim.40.b_join = f32[64,128]{1,0:T(8,128)} broadcast(f32[64]{0:T(128)S(1)} %get-tuple-element.25), dimensions={0} | broadcast | bytes 33024 | tf_op jit(solution)/shard_map/broadcast_in_dim | solution.py:208
  33.8 0.7 %broadcast_in_dim.42.b_first = f32[64,128]{1,0:T(8,128)} broadcast(f32[64]{0:T(128)S(1)} %get-tuple-element.24), dimensions={0} | broadcast | bytes 33024 | tf_op jit(solution)/shard_map/broadcast_in_dim | solution.py:208
  34.5 0.7 %broadcast_in_dim.44.b_second = f32[64,128]{1,0:T(8,128)} broadcast(f32[64]{0:T(128)S(1)} %get-tuple-element.23), dimensions={0} | broadcast | bytes 33024 | tf_op jit(solution)/shard_map/broadcast_in_dim | solution.py:208
  35.2 18.3 %shard_map.91 = (bf16[1,32,8,128]{3,2,1,0:T(8,128)(2,1)}, bf16[1,32,8,128]{3,2,1,0:T(8,128)(2,1)}, bf16[1,32,8,128]{3,2,1,0:T(8,128)(2,1)}, bf16[1,32,8,128]{3,2,1,0:T(8,128)(2,1)}) custom-call(s32[3]{0:T(128)} %pad_add_fusion.place, s32[1,4,8]{2,1,0:T(4,128)} %maximum_convert_fusion.flows, bf16[192,576]{1,0:T(8,128)(2,1)} %reshape.153.w_join, ...), custom_call_target="tpu_custom_call" | custom-call | tf_op jit(solution)/shard_map/pallas_call | solution.py:217
  53.5 1.0 %collective-permute-start.19 = (bf16[1,32,8,128]{3,2,1,0:T(8,128)(2,1)}, bf16[1,32,8,128]{3,2,1,0:T(8,128)(2,1)S(1)}, u32[]{:S(2)}, u32[]{:S(2)}) collective-permute-start(bf16[1,32,8,128]{3,2,1,0:T(8,128)(2,1)} %get-tuple-element.12), channel_id=1, source_target_pairs={{0,12},{4,0},{8,4},{12,8},{1,13},{5,1},{9,5},{13,9},{2,14},{6,2},{... | collective-permute-start | bytes 196616 | tf_op jit(solution)/shard_map/ppermute | solution.py:18
  54.6 1.0 %collective-permute-start.17 = (bf16[1,32,8,128]{3,2,1,0:T(8,128)(2,1)}, bf16[1,32,8,128]{3,2,1,0:T(8,128)(2,1)S(1)}, u32[]{:S(2)}, u32[]{:S(2)}) collective-permute-start(bf16[1,32,8,128]{3,2,1,0:T(8,128)(2,1)} %get-tuple-element.10), channel_id=1, source_target_pairs={{0,4},{4,8},{8,12},{12,0},{1,5},{5,9},{9,13},{13,1},{2,6},{6,10},{... | collective-permute-start | bytes 196616 | tf_op jit(solution)/shard_map/ppermute | solution.py:18
  55.6 2.4 %collective-permute-done.19 = bf16[1,32,8,128]{3,2,1,0:T(8,128)(2,1)S(1)} collective-permute-done((bf16[1,32,8,128]{3,2,1,0:T(8,128)(2,1)}, bf16[1,32,8,128]{3,2,1,0:T(8,128)(2,1)S(1)}, u32[]{:S(2)}, u32[]{:S(2)}) %collective-permute-start.19) | collective-permute-done | bytes 65568 | tf_op jit(solution)/shard_map/ppermute | solution.py:18
  58.0 4.3 %collective-permute-done.18 = bf16[1,32,8,128]{3,2,1,0:T(8,128)(2,1)S(1)} collective-permute-done((bf16[1,32,8,128]{3,2,1,0:T(8,128)(2,1)}, bf16[1,32,8,128]{3,2,1,0:T(8,128)(2,1)S(1)}, u32[]{:S(2)}, u32[]{:S(2)}) %collective-permute-start.18) | collective-permute-done | bytes 65568 | tf_op jit(solution)/shard_map/ppermute | solution.py:18
  62.3 0.9 %maximum_bitcast_fusion = bf16[4,32,8,128]{3,2,1,0:T(8,128)(2,1)S(1)} fusion(bf16[1,1,32,8,128]{4,3,2,1,0:T(8,128)(2,1)S(1)} %bitcast.57, bf16[1,1,32,8,128]{4,3,2,1,0:T(8,128)(2,1)S(1)} %bitcast.58, bf16[1,1,32,8,128]{4,3,2,1,0:T(8,128)(2,1)S(1)} %bitcast.59, bf16[1,1,32,8,128]{4,3,2,1,0:T(8,128)(2,1)} %bitcast.56), kind=kLoop, calls=%fused_computation.12 | loop fusion | flops 393216 | bytes 524288 | tf_op jit(solution)/shard_map/stack | solution.py:233
  63.2 0.6 gather_fusion
  63.8 0.8 %fusion.1 = bf16[4,1,32,8,128]{4,3,2,1,0:T(8,128)(2,1)} fusion(bf16[4,32,8,128]{3,2,1,0:T(8,128)(2,1)S(1)} %gather_fusion, pred[4]{0:T(512)(128)(4,1)S(1)} %compare_and_fusion), kind=kLoop, calls=%fused_computation.14 | loop fusion | flops 131072 | bytes 524292 | tf_op jit(solution)/shard_map/jit(_take)/select_n | solution.py:235
  (77 shorter events, 0.3 us)
Async XLA Ops:
  0.0 0.7 %copy-start.21 = (s32[4,2,1,2]{0,3,2,1:T(2,128)S(1)}, s32[4,2,1,2]{0,3,2,1:T(2,128)}, u32[]{:S(2)}) copy-start(s32[4,2,1,2]{0,3,2,1:T(2,128)} %param.11) | copy-start | bytes 196
  0.0 0.7 %copy-start.22 = (s32[4,2,1,2]{0,3,2,1:T(2,128)S(1)}, s32[4,2,1,2]{0,3,2,1:T(2,128)}, u32[]{:S(2)}) copy-start(s32[4,2,1,2]{0,3,2,1:T(2,128)} %param.10) | copy-start | bytes 196
  0.8 7.8 %copy-start.1 = (bf16[9,32,192]{2,1,0:T(8,128)(2,1)S(1)}, bf16[9,32,192]{2,1,0:T(8,128)(2,1)}, u32[]{:S(2)}) copy-start(bf16[9,32,192]{2,1,0:T(8,128)(2,1)} %param.12) | copy-start | bytes 331780
  0.9 7.8 %copy-start.2 = (bf16[1,9,32,64]{3,2,1,0:T(8,128)(2,1)S(1)}, bf16[1,9,32,64]{3,2,1,0:T(8,128)(2,1)}, u32[]{:S(2)}) copy-start(bf16[1,9,32,64]{3,2,1,0:T(8,128)(2,1)} %param.16) | copy-start | bytes 110596
  0.9 7.8 %copy-start.3 = (bf16[1,9,32,64]{3,2,1,0:T(8,128)(2,1)S(1)}, bf16[1,9,32,64]{3,2,1,0:T(8,128)(2,1)}, u32[]{:S(2)}) copy-start(bf16[1,9,32,64]{3,2,1,0:T(8,128)(2,1)} %param.14) | copy-start | bytes 110596
  1.9 7.6 %copy-start = (bf16[1,33,8,128]{3,2,1,0:T(8,128)(2,1)}, bf16[1,33,8,128]{3,2,1,0:T(8,128)(2,1)S(1)}, u32[]{:S(2)}) copy-start(bf16[1,33,8,128]{3,2,1,0:T(8,128)(2,1)S(1)} %get-tuple-element.17.rest_0_) | copy-start | bytes 202756
  1.9 22.4 %collective-permute-start.5 = (bf16[1,33,8,128]{3,2,1,0:T(8,128)(2,1)S(1)}, bf16[1,33,8,128]{3,2,1,0:T(8,128)(2,1)S(1)}, u32[]{:S(2)}, u32[]{:S(2)}) collective-permute-start(bf16[1,33,8,128]{3,2,1,0:T(8,128)(2,1)S(1)} %get-tuple-element.17.rest_0_), channel_id=1, source_target_pairs={{0,1},{1,0},{2,3},{3,2},{4,5},{5,4},{6,7},{7,6},{8,9},{9,8},{10,11... | collective-permute-start | bytes 202760 | tf_op jit(solution)/shard_map/ppermute | solution.py:18
  2.5 23.4 %collective-permute-start.9 = (bf16[1,33,8,128]{3,2,1,0:T(8,128)(2,1)S(1)}, bf16[1,33,8,128]{3,2,1,0:T(8,128)(2,1)S(1)}, u32[]{:S(2)}, u32[]{:S(2)}) collective-permute-start(bf16[1,33,8,128]{3,2,1,0:T(8,128)(2,1)S(1)} %get-tuple-element.17.rest_0_), channel_id=1, source_target_pairs={{0,2},{2,0},{1,3},{3,1},{4,6},{6,4},{5,7},{7,5},{8,10},{10,8},{9,1... | collective-permute-start | bytes 202760 | tf_op jit(solution)/shard_map/ppermute | solution.py:18
  5.0 17.2 %collective-permute-start.2 = (bf16[1,33,8,128]{3,2,1,0:T(8,128)(2,1)S(1)}, bf16[1,33,8,128]{3,2,1,0:T(8,128)(2,1)S(1)}, u32[]{:S(2)}, u32[]{:S(2)}) collective-permute-start(bf16[1,33,8,128]{3,2,1,0:T(8,128)(2,1)S(1)} %get-tuple-element.20), channel_id=1, source_target_pairs={{0,12},{4,0},{8,4},{12,8},{1,13},{5,1},{9,5},{13,9},{2,14},{6,2},{... | collective-permute-start | bytes 202760 | tf_op jit(solution)/shard_map/ppermute | solution.py:18
  8.8 0.7 %copy-start.18 = (f32[1,32]{1,0:T(1,128)S(1)}, f32[1,32]{1,0:T(1,128)}, u32[]{:S(2)}) copy-start(f32[1,32]{1,0:T(1,128)} %param.17) | copy-start | bytes 388
  8.8 0.7 %copy-start.19 = (f32[1,32]{1,0:T(1,128)S(1)}, f32[1,32]{1,0:T(1,128)}, u32[]{:S(2)}) copy-start(f32[1,32]{1,0:T(1,128)} %param.15) | copy-start | bytes 388
  8.8 0.7 %copy-start.20 = (f32[32]{0:T(128)S(1)}, f32[32]{0:T(128)}, u32[]{:S(2)}) copy-start(f32[32]{0:T(128)} %param.13) | copy-start | bytes 388
  8.8 14.5 %collective-permute-start.3 = (bf16[9,32,320]{2,1,0:T(8,128)(2,1)S(1)}, bf16[9,32,320]{2,1,0:T(8,128)(2,1)S(1)}, u32[]{:S(2)}, u32[]{:S(2)}) collective-permute-start(bf16[9,32,320]{2,1,0:T(8,128)(2,1)S(1)} %pad_maximum_fusion), channel_id=1, source_target_pairs={{0,1},{1,0},{2,3},{3,2},{4,5},{5,4},{6,7},{7,6},{8,9},{9,8},{10,11... | collective-permute-start | bytes 552968 | tf_op jit(solution)/shard_map/ppermute | solution.py:18
  9.5 1.2 %collective-permute-start.4 = (f32[3,32]{1,0:T(4,128)S(1)}, f32[3,32]{1,0:T(4,128)S(1)}, u32[]{:S(2)}, u32[]{:S(2)}) collective-permute-start(f32[3,32]{1,0:T(4,128)S(1)} %pad_maximum_fusion.3), channel_id=1, source_target_pairs={{0,1},{1,0},{2,3},{3,2},{4,5},{5,4},{6,7},{7,6},{8,9},{9,8},{10,11... | collective-permute-start | bytes 1160 | tf_op jit(solution)/shard_map/ppermute | solution.py:18
  10.7 6.3 %collective-permute-start = (bf16[1,33,8,128]{3,2,1,0:T(8,128)(2,1)S(1)}, bf16[1,33,8,128]{3,2,1,0:T(8,128)(2,1)S(1)}, u32[]{:S(2)}, u32[]{:S(2)}) collective-permute-start(bf16[1,33,8,128]{3,2,1,0:T(8,128)(2,1)S(1)} %get-tuple-element.18), channel_id=1, source_target_pairs={{0,4},{4,8},{8,12},{12,0},{1,5},{5,9},{9,13},{13,1},{2,6},{6,10},{... | collective-permute-start | bytes 202760 | tf_op jit(solution)/shard_map/ppermute | solution.py:18
  17.0 7.2 %copy-start.7 = (bf16[1,33,8,128]{3,2,1,0:T(8,128)(2,1)}, bf16[1,33,8,128]{3,2,1,0:T(8,128)(2,1)S(1)}, u32[]{:S(2)}) copy-start(bf16[1,33,8,128]{3,2,1,0:T(8,128)(2,1)S(1)} %collective-permute-done.rest_2_) | copy-start | bytes 202756
  17.0 5.2 %collective-permute-start.1 = (bf16[1,33,8,128]{3,2,1,0:T(8,128)(2,1)S(1)}, bf16[1,33,8,128]{3,2,1,0:T(8,128)(2,1)S(1)}, u32[]{:S(2)}, u32[]{:S(2)}) collective-permute-start(bf16[1,33,8,128]{3,2,1,0:T(8,128)(2,1)S(1)} %get-tuple-element.19), channel_id=1, source_target_pairs={{0,8},{4,12},{8,0},{12,4},{1,9},{5,13},{9,1},{13,5},{2,10},{6,14},... | collective-permute-start | bytes 202760 | tf_op jit(solution)/shard_map/ppermute | solution.py:18
  22.2 2.1 %copy-start.8 = (bf16[1,33,8,128]{3,2,1,0:T(8,128)(2,1)}, bf16[1,33,8,128]{3,2,1,0:T(8,128)(2,1)S(1)}, u32[]{:S(2)}) copy-start(bf16[1,33,8,128]{3,2,1,0:T(8,128)(2,1)S(1)} %collective-permute-done.1.rest_4_) | copy-start | bytes 202756
  22.2 6.6 %collective-permute-start.6 = (bf16[1,33,8,128]{3,2,1,0:T(8,128)(2,1)S(1)}, bf16[1,33,8,128]{3,2,1,0:T(8,128)(2,1)S(1)}, u32[]{:S(2)}, u32[]{:S(2)}) collective-permute-start(bf16[1,33,8,128]{3,2,1,0:T(8,128)(2,1)S(1)} %collective-permute-done.rest_2_), channel_id=1, source_target_pairs={{0,1},{1,0},{2,3},{3,2},{4,5},{5,4},{6,7},{7,6},{8,9},{9,8},{10,11... | collective-permute-start | bytes 202760 | tf_op jit(solution)/shard_map/ppermute | solution.py:18
  22.2 6.6 %copy-start.6 = (bf16[1,33,8,128]{3,2,1,0:T(8,128)(2,1)}, bf16[1,33,8,128]{3,2,1,0:T(8,128)(2,1)S(1)}, u32[]{:S(2)}) copy-start(bf16[1,33,8,128]{3,2,1,0:T(8,128)(2,1)S(1)} %collective-permute-done.2.rest_6_) | copy-start | bytes 202756
  22.2 6.6 %collective-permute-start.7 = (bf16[1,33,8,128]{3,2,1,0:T(8,128)(2,1)S(1)}, bf16[1,33,8,128]{3,2,1,0:T(8,128)(2,1)S(1)}, u32[]{:S(2)}, u32[]{:S(2)}) collective-permute-start(bf16[1,33,8,128]{3,2,1,0:T(8,128)(2,1)S(1)} %collective-permute-done.1.rest_4_), channel_id=1, source_target_pairs={{0,1},{1,0},{2,3},{3,2},{4,5},{5,4},{6,7},{7,6},{8,9},{9,8},{10,11... | collective-permute-start | bytes 202760 | tf_op jit(solution)/shard_map/ppermute | solution.py:18
  23.3 6.1 %collective-permute-start.11 = (bf16[1,33,8,128]{3,2,1,0:T(8,128)(2,1)S(1)}, bf16[1,33,8,128]{3,2,1,0:T(8,128)(2,1)}, u32[]{:S(2)}, u32[]{:S(2)}) collective-permute-start(bf16[1,33,8,128]{3,2,1,0:T(8,128)(2,1)S(1)} %collective-permute-done.rest_2_), channel_id=1, source_target_pairs={{0,2},{2,0},{1,3},{3,1},{4,6},{6,4},{5,7},{7,5},{8,10},{10,8},{9,1... | collective-permute-start | bytes 202760 | tf_op jit(solution)/shard_map/ppermute | solution.py:18
  24.3 2.4 %copy-start.4 = (bf16[1,33,8,128]{3,2,1,0:T(8,128)(2,1)}, bf16[1,33,8,128]{3,2,1,0:T(8,128)(2,1)S(1)}, u32[]{:S(2)}) copy-start(bf16[1,33,8,128]{3,2,1,0:T(8,128)(2,1)S(1)} %collective-permute-done.5.rest_1_) | copy-start | bytes 202756
  24.4 5.4 %collective-permute-start.13 = (bf16[1,33,8,128]{3,2,1,0:T(8,128)(2,1)S(1)}, bf16[1,33,8,128]{3,2,1,0:T(8,128)(2,1)S(1)}, u32[]{:S(2)}, u32[]{:S(2)}) collective-permute-start(bf16[1,33,8,128]{3,2,1,0:T(8,128)(2,1)S(1)} %collective-permute-done.1.rest_4_), channel_id=1, source_target_pairs={{0,2},{2,0},{1,3},{3,1},{4,6},{6,4},{5,7},{7,5},{8,10},{10,8},{9,1... | collective-permute-start | bytes 202760 | tf_op jit(solution)/shard_map/ppermute | solution.py:18
  25.9 2.9 %copy-start.5 = (bf16[1,33,8,128]{3,2,1,0:T(8,128)(2,1)}, bf16[1,33,8,128]{3,2,1,0:T(8,128)(2,1)S(1)}, u32[]{:S(2)}) copy-start(bf16[1,33,8,128]{3,2,1,0:T(8,128)(2,1)S(1)} %collective-permute-done.9.rest_8_) | copy-start | bytes 202756
  25.9 4.5 %collective-permute-start.15 = (bf16[1,33,8,128]{3,2,1,0:T(8,128)(2,1)S(1)}, bf16[1,33,8,128]{3,2,1,0:T(8,128)(2,1)S(1)}, u32[]{:S(2)}, u32[]{:S(2)}) collective-permute-start(bf16[1,33,8,128]{3,2,1,0:T(8,128)(2,1)S(1)} %collective-permute-done.2.rest_6_), channel_id=1, source_target_pairs={{0,2},{2,0},{1,3},{3,1},{4,6},{6,4},{5,7},{7,5},{8,10},{10,8},{9,1... | collective-permute-start | bytes 202760 | tf_op jit(solution)/shard_map/ppermute | solution.py:18
  28.8 1.9 %copy-start.9 = (bf16[1,33,8,128]{3,2,1,0:T(8,128)(2,1)}, bf16[1,33,8,128]{3,2,1,0:T(8,128)(2,1)S(1)}, u32[]{:S(2)}) copy-start(bf16[1,33,8,128]{3,2,1,0:T(8,128)(2,1)S(1)} %collective-permute-done.6.rest_3_) | copy-start | bytes 202756
  28.8 4.3 %collective-permute-start.8 = (bf16[1,33,8,128]{3,2,1,0:T(8,128)(2,1)S(1)}, bf16[1,33,8,128]{3,2,1,0:T(8,128)(2,1)S(1)}, u32[]{:S(2)}, u32[]{:S(2)}) collective-permute-start(bf16[1,33,8,128]{3,2,1,0:T(8,128)(2,1)S(1)} %collective-permute-done.2.rest_6_), channel_id=1, source_target_pairs={{0,1},{1,0},{2,3},{3,2},{4,5},{5,4},{6,7},{7,6},{8,9},{9,8},{10,11... | collective-permute-start | bytes 202760 | tf_op jit(solution)/shard_map/ppermute | solution.py:18
  28.9 1.8 %copy-start.10 = (bf16[1,33,8,128]{3,2,1,0:T(8,128)(2,1)}, bf16[1,33,8,128]{3,2,1,0:T(8,128)(2,1)S(1)}, u32[]{:S(2)}) copy-start(bf16[1,33,8,128]{3,2,1,0:T(8,128)(2,1)S(1)} %collective-permute-done.7.rest_5_) | copy-start | bytes 202756
  28.9 4.2 %collective-permute-start.10 = (bf16[1,33,8,128]{3,2,1,0:T(8,128)(2,1)S(1)}, bf16[1,33,8,128]{3,2,1,0:T(8,128)(2,1)S(1)}, u32[]{:S(2)}, u32[]{:S(2)}) collective-permute-start(bf16[1,33,8,128]{3,2,1,0:T(8,128)(2,1)S(1)} %collective-permute-done.9.rest_8_), channel_id=1, source_target_pairs={{0,1},{1,0},{2,3},{3,2},{4,5},{5,4},{6,7},{7,6},{8,9},{9,8},{10,11... | collective-permute-start | bytes 202760 | tf_op jit(solution)/shard_map/ppermute | solution.py:18
  29.4 3.6 %collective-permute-start.12 = (bf16[1,33,8,128]{3,2,1,0:T(8,128)(2,1)}, bf16[1,33,8,128]{3,2,1,0:T(8,128)(2,1)S(1)}, u32[]{:S(2)}, u32[]{:S(2)}) collective-permute-start(bf16[1,33,8,128]{3,2,1,0:T(8,128)(2,1)} %collective-permute-done.11.rest_10_), channel_id=1, source_target_pairs={{0,1},{1,0},{2,3},{3,2},{4,5},{5,4},{6,7},{7,6},{8,9},{9,8},{10,11... | collective-permute-start | bytes 202760 | tf_op jit(solution)/shard_map/ppermute | solution.py:18
  29.7 0.9 %copy-start.11 = (bf16[1,33,8,128]{3,2,1,0:T(8,128)(2,1)}, bf16[1,33,8,128]{3,2,1,0:T(8,128)(2,1)S(1)}, u32[]{:S(2)}) copy-start(bf16[1,33,8,128]{3,2,1,0:T(8,128)(2,1)S(1)} %collective-permute-done.13.rest_12_) | copy-start | bytes 202756
  29.7 3.4 %collective-permute-start.14 = (bf16[1,33,8,128]{3,2,1,0:T(8,128)(2,1)S(1)}, bf16[1,33,8,128]{3,2,1,0:T(8,128)(2,1)S(1)}, u32[]{:S(2)}, u32[]{:S(2)}) collective-permute-start(bf16[1,33,8,128]{3,2,1,0:T(8,128)(2,1)S(1)} %collective-permute-done.13.rest_12_), channel_id=1, source_target_pairs={{0,1},{1,0},{2,3},{3,2},{4,5},{5,4},{6,7},{7,6},{8,9},{9,8},{10,11... | collective-permute-start | bytes 202760 | tf_op jit(solution)/shard_map/ppermute | solution.py:18
  30.4 0.6 copy-start.12
  30.4 2.6 %collective-permute-start.16 = (bf16[1,33,8,128]{3,2,1,0:T(8,128)(2,1)S(1)}, bf16[1,33,8,128]{3,2,1,0:T(8,128)(2,1)S(1)}, u32[]{:S(2)}, u32[]{:S(2)}) collective-permute-start(bf16[1,33,8,128]{3,2,1,0:T(8,128)(2,1)S(1)} %collective-permute-done.15.rest_14_), channel_id=1, source_target_pairs={{0,1},{1,0},{2,3},{3,2},{4,5},{5,4},{6,7},{7,6},{8,9},{9,8},{10,11... | collective-permute-start | bytes 202760 | tf_op jit(solution)/shard_map/ppermute | solution.py:18
  33.0 2.1 %copy-start.13 = (bf16[1,33,8,128]{3,2,1,0:T(8,128)(2,1)}, bf16[1,33,8,128]{3,2,1,0:T(8,128)(2,1)S(1)}, u32[]{:S(2)}) copy-start(bf16[1,33,8,128]{3,2,1,0:T(8,128)(2,1)S(1)} %collective-permute-done.8.rest_7_) | copy-start | bytes 202756
  33.0 2.1 %copy-start.14 = (bf16[1,33,8,128]{3,2,1,0:T(8,128)(2,1)}, bf16[1,33,8,128]{3,2,1,0:T(8,128)(2,1)S(1)}, u32[]{:S(2)}) copy-start(bf16[1,33,8,128]{3,2,1,0:T(8,128)(2,1)S(1)} %collective-permute-done.10.rest_9_) | copy-start | bytes 202756
  33.1 2.1 %copy-start.15 = (bf16[1,33,8,128]{3,2,1,0:T(8,128)(2,1)}, bf16[1,33,8,128]{3,2,1,0:T(8,128)(2,1)S(1)}, u32[]{:S(2)}) copy-start(bf16[1,33,8,128]{3,2,1,0:T(8,128)(2,1)S(1)} %collective-permute-done.12.rest_11_) | copy-start | bytes 202756
  33.1 2.1 %copy-start.16 = (bf16[1,33,8,128]{3,2,1,0:T(8,128)(2,1)}, bf16[1,33,8,128]{3,2,1,0:T(8,128)(2,1)S(1)}, u32[]{:S(2)}) copy-start(bf16[1,33,8,128]{3,2,1,0:T(8,128)(2,1)S(1)} %collective-permute-done.14.rest_13_) | copy-start | bytes 202756
  33.1 2.1 %copy-start.17 = (bf16[1,33,8,128]{3,2,1,0:T(8,128)(2,1)}, bf16[1,33,8,128]{3,2,1,0:T(8,128)(2,1)S(1)}, u32[]{:S(2)}) copy-start(bf16[1,33,8,128]{3,2,1,0:T(8,128)(2,1)S(1)} %collective-permute-done.16.rest_15_) | copy-start | bytes 202756
  53.5 4.5 %collective-permute-start.19 = (bf16[1,32,8,128]{3,2,1,0:T(8,128)(2,1)}, bf16[1,32,8,128]{3,2,1,0:T(8,128)(2,1)S(1)}, u32[]{:S(2)}, u32[]{:S(2)}) collective-permute-start(bf16[1,32,8,128]{3,2,1,0:T(8,128)(2,1)} %get-tuple-element.12), channel_id=1, source_target_pairs={{0,12},{4,0},{8,4},{12,8},{1,13},{5,1},{9,5},{13,9},{2,14},{6,2},{... | collective-permute-start | bytes 196616 | tf_op jit(solution)/shard_map/ppermute | solution.py:18
  54.6 7.8 %collective-permute-start.18 = (bf16[1,32,8,128]{3,2,1,0:T(8,128)(2,1)}, bf16[1,32,8,128]{3,2,1,0:T(8,128)(2,1)S(1)}, u32[]{:S(2)}, u32[]{:S(2)}) collective-permute-start(bf16[1,32,8,128]{3,2,1,0:T(8,128)(2,1)} %get-tuple-element.11), channel_id=1, source_target_pairs={{0,8},{4,12},{8,0},{12,4},{1,9},{5,13},{9,1},{13,5},{2,10},{6,14},... | collective-permute-start | bytes 196616 | tf_op jit(solution)/shard_map/ppermute | solution.py:18
  54.6 7.8 %collective-permute-start.17 = (bf16[1,32,8,128]{3,2,1,0:T(8,128)(2,1)}, bf16[1,32,8,128]{3,2,1,0:T(8,128)(2,1)S(1)}, u32[]{:S(2)}, u32[]{:S(2)}) collective-permute-start(bf16[1,32,8,128]{3,2,1,0:T(8,128)(2,1)} %get-tuple-element.10), channel_id=1, source_target_pairs={{0,4},{4,8},{8,12},{12,0},{1,5},{5,9},{9,13},{13,1},{2,6},{6,10},{... | collective-permute-start | bytes 196616 | tf_op jit(solution)/shard_map/ppermute | solution.py:18
